TPU v7x, 32 devices: a whole 2x2x4 slice. The times are simulated.
32 devices in a mesh: batch: 8 (over z, x), mp: 4 (over y, core).
Axes of the slice: x: 2, y: 2, z: 4, core: 2. Of those that a mesh axis runs over, the one named last changes fastest.
Arguments:
- tokens: bfloat16 [16, 2048, 768], P('batch', 'mp'), may hold values from -6 to 6
- cotangent: bfloat16 [16, 2048, 768], P('batch', 'mp'), may hold values from -6 to 6
- lengths: int32 [16], P('batch'), may hold values from 64 to 2048, as said below
- pre_attn_gain: bfloat16 [768], replicated, may hold values from 0.099609375 to 1.8984375
- pre_attn_bias: bfloat16 [768], replicated, may hold values from -3 to 3
- qkv_weight: bfloat16 [3, 768, 768], replicated, may hold values from -0.21875 to 0.21875
- conv_weight: bfloat16 [3, 3, 768], replicated, may hold values from -3 to 3
- out_weight: bfloat16 [768, 768], replicated, may hold values from -1.5 to 1.5
- pre_ffn_gain: bfloat16 [768], replicated, may hold values from 0.099609375 to 1.8984375
- pre_ffn_bias: bfloat16 [768], replicated, may hold values from -3 to 3
- up_weight: bfloat16 [768, 3072], replicated, may hold values from -0.21875 to 0.21875
- up_bias: bfloat16 [3072], replicated, may hold values from -3 to 3
- down_weight: bfloat16 [3072, 768], replicated, may hold values from -0.109375 to 0.109375
- down_bias: bfloat16 [768], replicated, may hold values from -3 to 3
Outputs:
- output: bfloat16 [16, 2048, 768], P('batch', 'mp')
- tokens_grad: bfloat16 [16, 2048, 768], P('batch', 'mp')
- pre_attn_gain_grad: float32 [768], P(('batch', 'mp'))
- pre_attn_bias_grad: float32 [768], P(('batch', 'mp'))
- qkv_weight_grad: float32 [3, 768, 768], P(None, 'batch', 'mp')
- conv_weight_grad: float32 [3, 3, 768], P(None, None, ('batch', 'mp'))
- out_weight_grad: float32 [768, 768], P(('batch', 'mp'))
- pre_ffn_gain_grad: float32 [768], P(('batch', 'mp'))
- pre_ffn_bias_grad: float32 [768], P(('batch', 'mp'))
- up_weight_grad: float32 [768, 3072], P(('batch', 'mp'))
- up_bias_grad: float32 [3072], P(('batch', 'mp'))
- down_weight_grad: float32 [3072, 768], P(('batch', 'mp'))
- down_bias_grad: float32 [768], P(('batch', 'mp'))
Inputs may be any that keep to these rules, and one draw needn't show every extreme that they name: `lengths`: real tokens of each sequence; positions at or past it are padding. Some sequence has 2048 in every draw.
All inputs are finite; a program needn't handle non-finite values.
Results may differ from a plain program's by a relative error of at most 0.014.
The roundings to bfloat16 on the way count: a program that leaves them out, or rounds other values in their place, can miss the bound.
Values may be sent and summed in bfloat16 or wider, within the bound.
No kernel may reach another device: no remote copies, remote signals or barrier semaphores. Data moves between devices by JAX's collectives and lax.ppermute only.
A program may use at most 320 MiB of HBM per device.

v0:
```python
import functools
import itertools

import jax
import jax.numpy as jnp
from jax import lax
from jax.experimental import pallas as pl
from jax.experimental.pallas import tpu as pltpu
from jax.sharding import PartitionSpec as P

HEAD_DIM = 64
LANES = 128
EPSILON = 1e-05
NEGATIVE = -1000000000.0
QBLOCK = 512
KBLOCK = 256
F32 = jnp.float32
BF16 = jnp.bfloat16

CORE = [(i, i ^ 1) for i in range(4)]
PAIR = [(i, i ^ 2) for i in range(4)]


def dot_nt(left, right):
    return lax.dot_general(left, right, (((1,), (1,)), ((), ())), preferred_element_type=F32)


def dot_nn(left, right):
    return lax.dot_general(left, right, (((1,), (0,)), ((), ())), preferred_element_type=F32)


def dot_tn(left, right):
    return lax.dot_general(left, right, (((0,), (0,)), ((), ())), preferred_element_type=F32)


def params(mib):
    return pltpu.CompilerParams(vmem_limit_bytes=mib << 20)


def lane_tiles(values):
    return [values[:, n : n + LANES] for n in range(0, values.shape[1], LANES)]


def once(shape, index_map):
    return pl.BlockSpec(shape, index_map, pipeline_mode=pl.Buffered(1))


def still(array):
    return once(array.shape, lambda *_: (0,) * array.ndim)


CHEAP = pl.CostEstimate(flops=1 << 20, bytes_accessed=1 << 16, transcendentals=0)
SMEM_SPEC = pl.BlockSpec(memory_space=pltpu.SMEM)


def norm_stats(values):
    center = values - jnp.mean(values, axis=-1, keepdims=True)
    inv_std = lax.rsqrt(jnp.mean(center * center, axis=-1, keepdims=True) + EPSILON)
    return center * inv_std, inv_std


def norm_backward(grad_out, norm_gain, scaled, inv_std):
    weighted = grad_out * norm_gain
    return inv_std * (
        weighted
        - jnp.mean(weighted, axis=-1, keepdims=True)
        - scaled * jnp.mean(weighted * scaled, axis=-1, keepdims=True)
    )


def project_kernel(s_ref, x_ref, gain_ref, bias_ref, w_ref, normed_ref, proj_ref):
    scaled, _ = norm_stats(x_ref[...].astype(F32))
    normed = (scaled * gain_ref[...] + bias_ref[...]).astype(BF16)
    normed_ref[...] = normed.T
    for c in range(3):
        part = dot_nn(normed, w_ref[c]).astype(BF16)
        for n, tile in enumerate(lane_tiles(part)):
            start = (3 * n + c) * LANES
            proj_ref[:, start : start + LANES] = tile


def project(scalars, x, gain, bias, weights):
    rows, width = x.shape
    cols = 3 * width // 2
    return pl.pallas_call(
        project_kernel,
        grid_spec=pltpu.PrefetchScalarGridSpec(
            num_scalar_prefetch=1,
            grid=(1,),
            in_specs=[
                once((rows, width), lambda i, s: (0, 0)),
                once((1, width), lambda i, s: (0, 0)),
                once((1, width), lambda i, s: (0, 0)),
                once((3, width, width // 2), lambda i, s: (0, 0, s[0])),
            ],
            out_specs=[
                once((width, rows), lambda i, s: (0, 0)),
                once((rows, cols), lambda i, s: (0, 0)),
            ],
        ),
        out_shape=[
            jax.ShapeDtypeStruct((width, rows), BF16),
            jax.ShapeDtypeStruct((rows, cols), BF16),
        ],
        compiler_params=params(62),
        cost_estimate=CHEAP,
        name="project",
    )(scalars, x, gain, bias, weights)


def store_parts(flag, parts, keep_ref, send_ref):
    first = jnp.concatenate(parts[0], axis=0)
    second = jnp.concatenate(parts[1], axis=0)
    keep = jnp.where(flag == 0, first, second)
    send = jnp.where(flag == 0, second, first)
    keep_ref[...] = keep.astype(BF16).reshape(keep_ref.shape)
    send_ref[...] = send.astype(BF16).reshape(send_ref.shape)


def only_head(values, head):
    lane = lax.broadcasted_iota(jnp.int32, values.shape, 1)
    return jnp.where((lane // HEAD_DIM) == head, values, jnp.zeros_like(values))


def load_natural(member, blocks, dest, size, shift=0):
    for slot, block in enumerate(blocks):
        start = pl.multiple_of(lax.bitwise_xor(member, slot) * size, 8) + shift
        start = pl.multiple_of(start, 8)
        dest[pl.ds(start, size), :] = block.astype(dest.dtype)


def attend_kernel(
    m_ref, p0, p1, p2, p3, taps_ref, mixed_ref, own_ref, send_ref, lse_ref, pj, kh, vt, on, qs
):
    member = m_ref[1]
    size = p0.shape[0]
    length = 4 * size
    scale = jnp.asarray(HEAD_DIM ** (-0.5), BF16)
    for c in range(3):
        cols = slice(c * LANES, (c + 1) * LANES)
        pj[c, 0:8, :] = jnp.zeros((8, LANES), F32)
        load_natural(member, [p[:, cols] for p in (p0, p1, p2, p3)], pj.at[c], size, 8)
    for c in range(3):
        total = taps_ref[0, 3 * c : 3 * c + 1, :] * pj[c, 8 : 8 + length, :]
        total = total + taps_ref[0, 3 * c + 1 : 3 * c + 2, :] * pj[c, 7 : 7 + length, :]
        total = total + taps_ref[0, 3 * c + 2 : 3 * c + 3, :] * pj[c, 6 : 6 + length, :]
        mixed = total.astype(BF16)
        mixed_ref[:, c * LANES : (c + 1) * LANES] = mixed
        if c == 0:
            qs[...] = mixed * scale
        elif c == 1:
            kh[0] = only_head(mixed, 0)
            kh[1] = only_head(mixed, 1)
        else:
            vt[...] = mixed.T
    for first in range(0, length, QBLOCK):
        queries = qs[first : first + QBLOCK, :]
        keys = first + QBLOCK
        outs = []
        for head in range(2):
            scores = dot_nt(kh[head, 0:keys, :], queries)
            key_pos = lax.broadcasted_iota(jnp.int32, (QBLOCK, QBLOCK), 0)
            query_pos = lax.broadcasted_iota(jnp.int32, (QBLOCK, QBLOCK), 1)
            corner = jnp.where(key_pos <= query_pos, scores[first:keys, :], NEGATIVE)
            if first:
                scores = jnp.concatenate([scores[:first, :], corner], axis=0)
            else:
                scores = corner
            top = jnp.max(scores, axis=0, keepdims=True)
            weights = jnp.exp(scores - top)
            total = jnp.sum(weights, axis=0, keepdims=True)
            part = dot_nn(
                vt[head * HEAD_DIM : (head + 1) * HEAD_DIM, 0:keys], weights.astype(BF16)
            )
            outs.append(part * (1.0 / total))
            lse_ref[0, head : head + 1, first : first + QBLOCK] = top + jnp.log(total)
        on[first : first + QBLOCK, :] = jnp.concatenate(outs, axis=0).T.astype(BF16)
    for slot in range(4):
        start = pl.multiple_of(lax.bitwise_xor(member, slot) * size, size)
        block = on[pl.ds(start, size), :]
        dest = (own_ref, send_ref)[slot % 2]
        dest[slot // 2 * size : (slot // 2 + 1) * size, :] = block


def attend(member, proj, taps):
    size = proj[0].shape[0]
    pairs = proj[0].shape[1] // (3 * LANES)
    length = 4 * size
    width = pairs * LANES
    return pl.pallas_call(
        attend_kernel,
        grid=(pairs,),
        in_specs=[SMEM_SPEC]
        + [pl.BlockSpec((size, 3 * LANES), lambda p: (0, p))] * 4
        + [pl.BlockSpec((1, 16, LANES), lambda p: (p, 0, 0))],
        out_specs=[
            pl.BlockSpec((length, 3 * LANES), lambda p: (0, p)),
            pl.BlockSpec((2 * size, LANES), lambda p: (0, p)),
            pl.BlockSpec((2 * size, LANES), lambda p: (0, p)),
            pl.BlockSpec((1, 2, length), lambda p: (p, 0, 0)),
        ],
        out_shape=[
            jax.ShapeDtypeStruct((length, 3 * width), BF16),
            jax.ShapeDtypeStruct((2 * size, width), BF16),
            jax.ShapeDtypeStruct((2 * size, width), BF16),
            jax.ShapeDtypeStruct((pairs, 2, length), F32),
        ],
        scratch_shapes=[
            pltpu.VMEM((3, 8 + length, LANES), F32),
            pltpu.VMEM((2, length, LANES), BF16),
            pltpu.VMEM((LANES, length), BF16),
            pltpu.VMEM((length, LANES), BF16),
            pltpu.VMEM((length, LANES), BF16),
        ],
        compiler_params=params(62),
        cost_estimate=CHEAP,
        name="attend",
    )(member, *proj, taps)


def attend_back_kernel(
    m_ref,
    p0,
    p1,
    p2,
    p3,
    mixed_ref,
    lse_ref,
    taps_ref,
    own_ref,
    send_ref,
    down_ref,
    drecv_ref,
    n0,
    n1,
    n2,
    n3,
    gown_ref,
    gsend_ref,
    gconv_ref,
    keep_ref,
    give_ref,
    pj,
    dm,
    qh,
    doh,
    kt,
    dl,
    dqa,
    nat,
    gp,
):
    member = m_ref[1]
    size = p0.shape[0]
    length = 4 * size
    scale = jnp.asarray(HEAD_DIM ** (-0.5), BF16)
    halves = [slice(0, size), slice(size, 2 * size)]
    load_natural(
        member,
        [own_ref[halves[0]], send_ref[halves[0]], own_ref[halves[1]], send_ref[halves[1]]],
        nat.at[0],
        size,
    )
    load_natural(
        member,
        [down_ref[halves[0]], drecv_ref[halves[0]], down_ref[halves[1]], drecv_ref[halves[1]]],
        nat.at[1],
        size,
    )
    grads = nat[1]
    product = (grads.astype(F32) * nat[0].astype(F32)).T
    for head in range(2):
        dl[head : head + 1, :] = jnp.sum(
            product[head * HEAD_DIM : (head + 1) * HEAD_DIM, :], axis=0, keepdims=True
        )
        doh[head] = only_head(grads, head)
        qh[head] = only_head(mixed_ref[:, 0:LANES], head) * scale
    kt[...] = mixed_ref[:, LANES : 2 * LANES].T
    for c in range(3):
        cols = slice(c * LANES, (c + 1) * LANES)
        pj[c, 0:8, :] = jnp.zeros((8, LANES), F32)
        dm[c, length : length + 8, :] = jnp.zeros((8, LANES), F32)
        load_natural(member, [p[:, cols] for p in (p0, p1, p2, p3)], pj.at[c], size, 8)
    for first in range(0, length, KBLOCK):
        keys = mixed_ref[first : first + KBLOCK, LANES : 2 * LANES]
        values = mixed_ref[first : first + KBLOCK, 2 * LANES : 3 * LANES]
        sum_v = None
        sum_k = None
        for head in range(2):
            scores = dot_nt(keys, qh[head, first:, :])
            key_pos = lax.broadcasted_iota(jnp.int32, (KBLOCK, KBLOCK), 0)
            query_pos = lax.broadcasted_iota(jnp.int32, (KBLOCK, KBLOCK), 1)
            corner = jnp.where(key_pos <= query_pos, scores[:, :KBLOCK], NEGATIVE)
            if first + KBLOCK < length:
                scores = jnp.concatenate([corner, scores[:, KBLOCK:]], axis=1)
            else:
                scores = corner
            probs = jnp.exp(scores - lse_ref[0, head : head + 1, first:])
            grad_probs = dot_nt(values, doh[head, first:, :])
            grad_scores = (probs * (grad_probs - dl[head : head + 1, first:])).astype(BF16)
            part_v = dot_nn(probs.astype(BF16), doh[head, first:, :])
            part_k = dot_nn(grad_scores, qh[head, first:, :])
            sum_v = part_v if sum_v is None else sum_v + part_v
            sum_k = part_k if sum_k is None else sum_k + part_k
            lanes = slice(head * HEAD_DIM, (head + 1) * HEAD_DIM)
            part_q = dot_nn(kt[lanes, first : first + KBLOCK], grad_scores)
            if first == 0:
                dqa[lanes, :] = part_q
            else:
                dqa[lanes, first:] += part_q
        dm[1, first : first + KBLOCK, :] = sum_k
        dm[2, first : first + KBLOCK, :] = sum_v
    dm[0, 0:length, :] = dqa[...].T * HEAD_DIM ** (-0.5)
    for c in range(3):
        grad = dm[c, 0:length, :]
        for s in range(3):
            gconv_ref[3 * c + s : 3 * c + s + 1, :] = jnp.sum(
                grad * pj[c, 8 - s : 8 - s + length, :], axis=0, keepdims=True
            )
        total = taps_ref[0, 3 * c : 3 * c + 1, :] * grad
        total = total + taps_ref[0, 3 * c + 1 : 3 * c + 2, :] * dm[c, 1 : 1 + length, :]
        total = total + taps_ref[0, 3 * c + 2 : 3 * c + 3, :] * dm[c, 2 : 2 + length, :]
        gp[:, c * LANES : (c + 1) * LANES] = total.astype(BF16)
    total = None
    for slot, norm in enumerate((n0, n1, n2, n3)):
        start = pl.multiple_of(lax.bitwise_xor(member, slot) * size, size)
        dest = (gown_ref, gsend_ref)[slot % 2]
        block = gp[pl.ds(start, size), :]
        dest[slot // 2 * size : (slot // 2 + 1) * size, :] = block
        part = dot_nn(norm[...], block)
        total = part if total is None else total + part
    rows = total.shape[0] // 8
    store_parts(
        m_ref[3],
        [
            [
                tile
                for b in (x, x + 4, x + 2, x + 6)
                for tile in lane_tiles(total[b * rows : (b + 1) * rows])
            ]
            for x in range(2)
        ],
        keep_ref,
        give_ref,
    )


def attend_back(pair, member, proj, mixed, lse, taps, own, send, grad_own, grad_recv, normed):
    size = proj[0].shape[0]
    length = 4 * size
    width = normed[0].shape[0]
    part = jax.ShapeDtypeStruct((2, 2, 3 * width // 8, LANES), BF16)
    half_spec = pl.BlockSpec((2 * size, LANES), lambda i: (0, pair))
    return pl.pallas_call(
        attend_back_kernel,
        grid=(1,),
        in_specs=[SMEM_SPEC]
        + [pl.BlockSpec((size, 3 * LANES), lambda i: (0, pair))] * 4
        + [
            pl.BlockSpec((length, 3 * LANES), lambda i: (0, pair)),
            pl.BlockSpec((1, 2, length), lambda i: (pair, 0, 0)),
            pl.BlockSpec((1, 16, LANES), lambda i: (pair, 0, 0)),
        ]
        + [half_spec] * 4
        + [pl.BlockSpec((width, size), lambda i: (0, 0))] * 4,
        out_specs=[
            pl.BlockSpec((2 * size, 3 * LANES), lambda i: (0, 0)),
            pl.BlockSpec((2 * size, 3 * LANES), lambda i: (0, 0)),
            pl.BlockSpec((16, LANES), lambda i: (0, 0)),
            pl.BlockSpec(part.shape, lambda i: (0, 0, 0, 0)),
            pl.BlockSpec(part.shape, lambda i: (0, 0, 0, 0)),
        ],
        out_shape=[
            jax.ShapeDtypeStruct((2 * size, 3 * LANES), BF16),
            jax.ShapeDtypeStruct((2 * size, 3 * LANES), BF16),
            jax.ShapeDtypeStruct((16, LANES), F32),
            part,
            part,
        ],
        scratch_shapes=[
            pltpu.VMEM((3, 8 + length, LANES), F32),
            pltpu.VMEM((3, 8 + length, LANES), F32),
            pltpu.VMEM((2, length, LANES), BF16),
            pltpu.VMEM((2, length, LANES), BF16),
            pltpu.VMEM((LANES, length), BF16),
            pltpu.VMEM((8, length), F32),
            pltpu.VMEM((LANES, length), F32),
            pltpu.VMEM((2, length, LANES), BF16),
            pltpu.VMEM((length, 3 * LANES), BF16),
        ],
        compiler_params=params(62),
        cost_estimate=CHEAP,
        name="attend_back",
    )(member, *proj, mixed, lse, taps, own, send, grad_own, grad_recv, *normed)


def canonical(flag, own_ref, recv_ref):
    own = own_ref[...]
    recv = recv_ref[...]
    return jnp.concatenate(
        [jnp.where(flag == 0, own, recv), jnp.where(flag == 0, recv, own)], axis=1
    )


def ffn_forward_kernel(
    s_ref,
    hown_ref,
    hrecv_ref,
    wout_ref,
    tok0,
    tok1,
    cot0,
    cot1,
    gain_ref,
    bias_ref,
    up_ref,
    upb_ref,
    down_ref,
    downb_ref,
    res_ref,
    nf_ref,
    gf_ref,
    relu_ref,
    out0,
    out1,
    dbias_ref,
    keep_ref,
    send_ref,
    acc,
):
    step = pl.program_id(0)
    size = tok0.shape[0]
    core = s_ref[0]
    halves = ((0, s_ref[1] * size), (size, lax.bitwise_xor(s_ref[1], 2) * size))

    def valid(start):
        row = start + lax.broadcasted_iota(jnp.int32, tok0.shape, 0)
        return row < s_ref[2]

    @pl.when(step == 0)
    def _():
        attended = dot_nn(canonical(core, hown_ref, hrecv_ref), wout_ref[...])
        for tok, cot, (first, start) in zip((tok0, tok1), (cot0, cot1), halves):
            rows = slice(first, first + size)
            residual = tok[...].astype(F32) + attended[rows]
            res_ref[rows, :] = residual
            scaled, _ = norm_stats(residual)
            nf_ref[rows, :] = (scaled * gain_ref[...] + bias_ref[...]).astype(BF16)
            grad = cot[...]
            gf_ref[rows, :] = jnp.where(valid(start), grad, jnp.zeros_like(grad))
        dbias_ref[0:1, :] = jnp.sum(gf_ref[...].astype(F32), axis=0, keepdims=True)
        acc[...] = jnp.zeros_like(acc)

    relu = jnp.maximum(dot_nn(nf_ref[...], up_ref[...]) + upb_ref[...], 0.0)
    relu_ref[...] = relu
    act = (relu * relu).astype(BF16)
    acc[...] += dot_nn(act, down_ref[...])
    grad = dot_tn(act, gf_ref[...])
    rows = grad.shape[0] // 8
    store_parts(
        core,
        [
            [
                tile
                for chunk in (bit, bit + 4, bit + 2, bit + 6)
                for tile in lane_tiles(grad[chunk * rows : (chunk + 1) * rows])
            ]
            for bit in range(2)
        ],
        keep_ref,
        send_ref,
    )

    @pl.when(step == pl.num_programs(0) - 1)
    def _():
        for out, (first, start) in zip((out0, out1), halves):
            rows = slice(first, first + size)
            total = res_ref[rows, :] + (acc[rows, :] + downb_ref[...])
            out[...] = jnp.where(valid(start), total, 0.0).astype(BF16).reshape(out.shape)


def ffn_forward(scalars, hown, hrecv, wout, toks, cots, gain, bias, up, upb, down, downb):
    rows = 2 * toks[0].shape[0]
    width, ff = up.shape
    tile = ff // 4
    part = jax.ShapeDtypeStruct((2, 2, 2, 2, tile // 8 * width // LANES, LANES), BF16)
    part_spec = pl.BlockSpec(
        (2, 2, 1, 1) + part.shape[4:], lambda j, _: (0, 0, lax.rem(j, 2), lax.div(j, 2), 0, 0)
    )
    full = lambda dtype: jax.ShapeDtypeStruct((rows, width), dtype)
    block = jax.ShapeDtypeStruct(toks[0].shape, BF16)
    return pl.pallas_call(
        ffn_forward_kernel,
        grid_spec=pltpu.PrefetchScalarGridSpec(
            num_scalar_prefetch=1,
            grid=(4,),
            in_specs=[still(a) for a in (hown, hrecv, wout, *toks, *cots, gain, bias)]
            + [
                pl.BlockSpec((width, tile), lambda j, _: (0, j)),
                pl.BlockSpec((1, tile), lambda j, _: (0, j)),
                pl.BlockSpec((tile, width), lambda j, _: (j, 0)),
                still(downb),
            ],
            out_specs=[once((rows, width), lambda j, _: (0, 0))] * 3
            + [
                pl.BlockSpec((rows, tile), lambda j, _: (0, j)),
                once((1,) + block.shape, lambda j, s: (s[4], 0, 0)),
                once(block.shape, lambda j, _: (0, 0)),
                pl.BlockSpec((8, width), lambda j, _: (0, 0)),
                part_spec,
                part_spec,
            ],
            scratch_shapes=[pltpu.VMEM((rows, width), F32)],
        ),
        out_shape=[
            full(F32),
            full(BF16),
            full(BF16),
            jax.ShapeDtypeStruct((rows, ff), F32),
            jax.ShapeDtypeStruct((2,) + block.shape, BF16),
            block,
            jax.ShapeDtypeStruct((8, width), F32),
            part,
            part,
        ],
        compiler_params=params(60),
        cost_estimate=CHEAP,
        name="ffn_forward",
    )(scalars, hown, hrecv, wout, *toks, *cots, gain, bias, up, upb, down, downb)


def ffn_backward_kernel(
    s_ref,
    gf_ref,
    nf_ref,
    res_ref,
    hown_ref,
    hrecv_ref,
    wout_ref,
    gain_ref,
    dbias_ref,
    relu_ref,
    up_ref,
    down_ref,
    gres_ref,
    gown_ref,
    gsend_ref,
    sums_ref,
    keep_ref,
    send_ref,
    nft,
    gn,
):
    step = pl.program_id(0)
    last = pl.num_programs(0) - 1
    core = s_ref[0]

    def store(grad):
        rows = grad.shape[0] // 32
        store_parts(
            core,
            [
                [
                    tile
                    for place in range(16)
                    for chunk in [
                        bit
                        + (place >> 3 & 1) * 2
                        + (place >> 2 & 1) * 4
                        + (place >> 1 & 1) * 8
                        + (place & 1) * 16
                    ]
                    for tile in lane_tiles(grad[chunk * rows : (chunk + 1) * rows])
                ]
                for bit in range(2)
            ],
            keep_ref,
            send_ref,
        )

    @pl.when(step == 0)
    def _():
        nft[...] = nf_ref[...].T
        gn[...] = jnp.zeros_like(gn)

    @pl.when(step < last)
    def _():
        grad_act = dot_nt(gf_ref[...], down_ref[...])
        grad_pre = (2.0 * relu_ref[...] * grad_act).astype(BF16)
        sums_ref[pl.ds(step, 1), :] = jnp.sum(grad_pre.astype(F32), axis=0, keepdims=True)
        gn[...] += dot_nt(grad_pre, up_ref[...])
        store(dot_nn(nft[...], grad_pre))

    @pl.when(step == last)
    def _():
        scaled, inv_std = norm_stats(res_ref[...])
        grad = gn[...]
        sums_ref[4:5, :] = jnp.sum(grad * scaled, axis=0, keepdims=True)
        sums_ref[5:6, :] = jnp.sum(grad, axis=0, keepdims=True)
        sums_ref[6:7, :] = dbias_ref[0:1, :]
        sums_ref[7:8, :] = jnp.zeros_like(sums_ref[7:8, :])
        total = gf_ref[...].astype(F32) + norm_backward(grad, gain_ref[...], scaled, inv_std)
        gres_ref[...] = total
        attended = total.astype(BF16)
        heads = dot_nt(attended, wout_ref[...]).astype(BF16)
        middle = heads.shape[1] // 2
        gown_ref[...] = jnp.where(core == 0, heads[:, :middle], heads[:, middle:])
        gsend_ref[...] = jnp.where(core == 0, heads[:, middle:], heads[:, :middle])
        store(dot_tn(canonical(core, hown_ref, hrecv_ref), attended))


def ffn_backward(scalars, gf, nf, res, hown, hrecv, wout, gain, dbias, relu, up, down):
    rows, width = nf.shape
    ff = up.shape[1]
    tile = ff // 4
    block = width // 32 * tile // LANES
    part = jax.ShapeDtypeStruct((2, 2, 2, 2, 5 * block, LANES), BF16)
    part_spec = pl.BlockSpec((2, 2, 2, 2, block, LANES), lambda j: (0, 0, 0, 0, j, 0))
    now = lambda j: jnp.minimum(j, 3)
    half = jax.ShapeDtypeStruct(hown.shape, BF16)
    return pl.pallas_call(
        ffn_backward_kernel,
        grid=(5,),
        in_specs=[SMEM_SPEC]
        + [still(a) for a in (gf, nf, res, hown, hrecv, wout, gain, dbias)]
        + [
            pl.BlockSpec((rows, tile), lambda j: (0, now(j))),
            pl.BlockSpec((width, tile), lambda j: (0, now(j))),
            pl.BlockSpec((tile, width), lambda j: (now(j), 0)),
        ],
        out_specs=[once((rows, width), lambda j: (0, 0))]
        + [once(half.shape, lambda j: (0, 0))] * 2
        + [
            pl.BlockSpec((8, width), lambda j: (0, 0)),
            part_spec,
            part_spec,
        ],
        out_shape=[
            jax.ShapeDtypeStruct((rows, width), F32),
            half,
            half,
            jax.ShapeDtypeStruct((8, width), F32),
            part,
            part,
        ],
        scratch_shapes=[pltpu.VMEM((width, rows), BF16), pltpu.VMEM((rows, width), F32)],
        compiler_params=params(60),
        cost_estimate=CHEAP,
        name="ffn_backward",
    )(scalars, gf, nf, res, hown, hrecv, wout, gain, dbias, relu, up, down)


def input_grad_kernel(
    final, s_ref, o0, o1, o2, r0, r1, r2, w_ref, x_ref, gres_ref, gain_ref, *refs
):
    out_ref, sums_ref, buf = refs[-3:]
    for n, ref in enumerate((o0, o1, o2, r0, r1, r2)):
        side = s_ref[0] if n < 3 else 1 - s_ref[0]
        start = pl.multiple_of((side * 3 + n % 3) * LANES, LANES)
        for c, tile in enumerate(lane_tiles(ref[...])):
            buf[c, :, pl.ds(start, LANES)] = tile
    grad = dot_nt(buf[0], w_ref[0]) + dot_nt(buf[1], w_ref[1]) + dot_nt(buf[2], w_ref[2])
    scaled, inv_std = norm_stats(x_ref[...].astype(F32))
    first = 17 if final else 0

    @pl.when(pl.program_id(0) == 0)
    def _():
        sums_ref[...] = jnp.zeros_like(sums_ref)
        if final:
            early_ref, before_ref, *convs = refs[:-3]
            sums_ref[0:8, :] = early_ref[...]
            sums_ref[first : first + 2, :] = before_ref[0:2, :]
            for n, conv in enumerate(convs):
                start = pl.multiple_of((s_ref[0] * 3 + n) * LANES, LANES)
                sums_ref[8:17, pl.ds(start, LANES)] = conv[0:9, :]

    sums_ref[first : first + 1, :] += jnp.sum(grad * scaled, axis=0, keepdims=True)
    sums_ref[first + 1 : first + 2, :] += jnp.sum(grad, axis=0, keepdims=True)
    total = gres_ref[...] + norm_backward(grad, gain_ref[...], scaled, inv_std)
    out_ref[...] = total.astype(BF16).reshape(out_ref.shape)


def input_grad(slot, scalars, owns, recvs, weights, x, grad_residual, gain, small=()):
    rows, width = x.shape
    tile = rows // 2
    final = len(small) > 0
    part = pl.BlockSpec((tile, 3 * LANES), lambda i, _: (2 * slot + i, 0))
    if final:
        out_spec = pl.BlockSpec((1, tile, width), lambda i, s: (s[4], i, 0))
        out = jax.ShapeDtypeStruct((2, rows, width), BF16)
    else:
        out_spec = pl.BlockSpec((tile, width), lambda i, _: (i, 0))
        out = jax.ShapeDtypeStruct((rows, width), BF16)
    sums = jax.ShapeDtypeStruct((24 if final else 8, width), F32)
    return pl.pallas_call(
        functools.partial(input_grad_kernel, final),
        grid_spec=pltpu.PrefetchScalarGridSpec(
            num_scalar_prefetch=1,
            grid=(2,),
            in_specs=[part] * 6
            + [
                still(weights),
                pl.BlockSpec((tile, width), lambda i, _: (i, 0)),
                pl.BlockSpec((tile, width), lambda i, _: (2 * slot + i, 0)),
                still(gain),
            ]
            + [still(a) for a in small],
            out_specs=[out_spec, pl.BlockSpec(sums.shape, lambda i, _: (0, 0))],
            scratch_shapes=[pltpu.VMEM((3, tile, width), BF16)],
        ),
        out_shape=[out, sums],
        compiler_params=params(62),
        cost_estimate=CHEAP,
        name="input_grad",
    )(scalars, *owns, *recvs, weights, x, grad_residual, gain, *small)


FREE, ONE, MINE, OTHER = range(4)
BIT_AT = (4, 3, 5, 6)


class Segment:
    def __init__(self, arrays, first, rows):
        self.rows = rows
        self.parts = [(array, self.fresh(array), first) for array in arrays]

    @staticmethod
    def fresh(array):
        return [FREE if n == 2 else ONE for n in array.shape[:4]]

    def chosen(self, dim):
        found = []
        for array, marks, first in self.parts:
            marks = list(marks)
            if dim is not None and marks[dim] == FREE:
                marks[dim] = OTHER
            found.append((array, tuple(marks), first, self.rows))
        return found

    def settle(self, dim, arrived, first):
        parts = []
        for array, marks, own_first in self.parts:
            marks = list(marks)
            if marks[dim] == FREE:
                marks[dim] = MINE
            parts.append((array, marks, own_first))
        self.parts = parts + [(arrived, self.fresh(arrived), first)]


def settle(segments, dim, arrived):
    first = 0
    for segment in segments:
        segment.settle(dim, arrived, first)
        first += segment.rows


def sum_kernel(plan, finish, count, s_ref, *refs):
    pieces = [p for parts in plan for p in parts]
    arrays, outs = refs[:count], refs[count : len(refs) - len(pieces) - 1]
    bufs, sems = refs[len(refs) - len(pieces) - 1 : -1], refs[-1]
    copies = []
    for n, (place, marks, first, rows) in enumerate(pieces):
        where = []
        for dim, mark in enumerate(marks):
            bit = s_ref[BIT_AT[dim]]
            start = {FREE: 0, ONE: 0, MINE: bit, OTHER: 1 - bit}[mark]
            where.append(pl.ds(start, 2 if mark == FREE else 1))
        source = arrays[place].at[tuple(where) + (pl.ds(first, rows), slice(None))]
        copies.append(pltpu.make_async_copy(source, bufs[n], sems.at[n]))
        copies[-1].start()
    n = 0
    totals = []
    for parts in plan:
        for copy in copies[n : n + len(parts)]:
            copy.wait()
        own = bufs[n : n + len(parts)]
        n += len(parts)

        def total(lead, rows, own=own):
            value = None
            for buf in own:
                piece = buf[lead + (rows, slice(None))].astype(F32)
                value = piece if value is None else value + piece
            return value

        totals.append(total)
    finish(s_ref, totals, outs)


def sum_call(scalars, segments, dims, finish, out_shape, name):
    arrays, plan, scratch = [], [], []
    for segment, dim in zip(segments, dims):
        parts = []
        for array, marks, first, rows in segment.chosen(dim):
            place = next((n for n, a in enumerate(arrays) if a is array), None)
            if place is None:
                place = len(arrays)
                arrays.append(array)
            parts.append((place, marks, first, rows))
            sizes = tuple(2 if mark == FREE else 1 for mark in marks)
            scratch.append(pltpu.VMEM(sizes + (rows, LANES), BF16))
        plan.append(parts)
    whole = lambda shape: pl.BlockSpec(shape, lambda i: (0,) * len(shape))
    return pl.pallas_call(
        functools.partial(sum_kernel, plan, finish, len(arrays)),
        grid=(1,),
        in_specs=[SMEM_SPEC] + [pl.BlockSpec(memory_space=pltpu.HBM)] * len(arrays),
        out_specs=[whole(o.shape) for o in out_shape],
        out_shape=out_shape,
        scratch_shapes=scratch + [pltpu.SemaphoreType.DMA((len(scratch),))],
        compiler_params=params(62),
        cost_estimate=CHEAP,
        name=name,
    )(scalars, *arrays)


def outgoing(scalars, groups, dims, name="stage_sum"):
    shapes = []
    for group, dim in zip(groups, dims):
        marks = [group[0].chosen(dim)[0][1]]
        sizes = tuple(2 if mark == FREE else 1 for mark in marks[0])
        shapes.append(jax.ShapeDtypeStruct(sizes + (sum(g.rows for g in group), LANES), BF16))

    def finish(s_ref, totals, outs):
        n = 0
        for group, out in zip(groups, outs):
            first = 0
            for segment in group:
                for lead in itertools.product(*[range(size) for size in out.shape[:4]]):
                    for row in range(0, segment.rows, 48):
                        value = totals[n](lead, slice(row, row + 48))
                        out[lead + (slice(first + row, first + row + 48), slice(None))] = (
                            value.astype(BF16)
                        )
                first += segment.rows
                n += 1

    segments = [segment for group in groups for segment in group]
    each = [dim for group, dim in zip(groups, dims) for _ in group]
    return sum_call(scalars, segments, each, finish, shapes, name)


def hop(value, stage):
    return lax.ppermute(value, stage[0], stage[1])


def ffn_plain(heads, toks, cot, valid, wout, gain, bias, up, upb, down, downb):
    residual = toks.astype(F32) + jnp.dot(heads, wout, preferred_element_type=F32)
    scaled, inv_std = norm_stats(residual)
    normed = (scaled * gain + bias).astype(BF16)
    relu = jnp.maximum(jnp.dot(normed, up, preferred_element_type=F32) + upb, 0.0)
    act = jnp.square(relu).astype(BF16)
    out = jnp.dot(act, down, preferred_element_type=F32) + downb
    result = jnp.where(valid, residual + out, 0.0).astype(BF16)
    grad_ffn = jnp.where(valid, cot, jnp.zeros_like(cot))
    grad_y = grad_ffn.astype(F32)
    grad_act = jnp.einsum("td,fd->tf", grad_ffn, down, preferred_element_type=F32)
    grad_pre = (2.0 * relu * grad_act).astype(BF16)
    grad = jnp.einsum("tf,df->td", grad_pre, up, preferred_element_type=F32)
    sums = jnp.stack([jnp.sum(grad * scaled, axis=0), jnp.sum(grad, axis=0)])
    grad_residual = grad_y + norm_backward(grad, gain, scaled, inv_std)
    attended = grad_residual.astype(BF16)
    grad_heads = jnp.einsum("td,ed->te", attended, wout, preferred_element_type=F32)
    return (
        result,
        grad_residual,
        grad_heads.astype(BF16),
        sums,
        jnp.sum(grad_pre.astype(F32), axis=0),
        jnp.sum(grad_y, axis=0),
        jnp.einsum("td,tf->df", normed, grad_pre, preferred_element_type=F32),
        jnp.einsum("tf,td->fd", act, grad_ffn, preferred_element_type=F32),
        jnp.einsum("te,td->ed", heads, attended, preferred_element_type=F32),
    )


def on_device(
    tokens,
    cotangent,
    lengths,
    pre_attn_gain,
    pre_attn_bias,
    qkv_weight,
    conv_weight,
    out_weight,
    pre_ffn_gain,
    pre_ffn_bias,
    up_weight,
    up_bias,
    down_weight,
    down_bias,
):
    groups = lax.axis_size("mp")
    batch_groups = lax.axis_size("batch")
    devices = groups * batch_groups
    member = lax.axis_index("mp").astype(jnp.int32)
    batch = lax.axis_index("batch").astype(jnp.int32)
    seqs, rows, width = tokens.shape
    ff = up_weight.shape[1]
    middle = width // 2
    quarter = width // groups
    pairs = middle // LANES
    taps = conv_weight.shape[1]
    assert groups == 4 and seqs == 2 and pairs == 3 and taps == 3
    fast = batch_groups == 8 and (width // devices) % 8 == 0
    half = lax.shift_right_logical(member, 1)
    core = lax.bitwise_and(member, 1)
    x_bit = lax.bitwise_and(batch, 1)
    z0_bit = lax.bitwise_and(lax.shift_right_logical(batch, 1), 1)
    z1_bit = lax.shift_right_logical(batch, 2)
    gain_attn = pre_attn_gain.astype(F32).reshape(1, width)
    bias_attn = pre_attn_bias.astype(F32).reshape(1, width)
    gain_ffn = pre_ffn_gain.astype(F32).reshape(1, width)
    bias_ffn = pre_ffn_bias.astype(F32).reshape(1, width)
    up_bias_f = up_bias.astype(F32).reshape(1, ff)
    down_bias_f = down_bias.astype(F32).reshape(1, width)

    def swap_core(value):
        return lax.ppermute(value, "mp", CORE)

    def swap_pair(value):
        return lax.ppermute(value, "mp", PAIR)

    def pick(value, index):
        starts = (index,) + (jnp.int32(0),) * (value.ndim - 1)
        return lax.dynamic_slice(value, starts, (1,) + value.shape[1:])[0]

    length = pick(lengths, half)
    scalars = jnp.stack([core, member, length, x_bit, half, z0_bit, z1_bit]).astype(jnp.int32)

    hops = [("mp", PAIR)] + [
        ("batch", [(i, i ^ flip) for i in range(batch_groups)]) for flip in (1, 2, 4)
    ]
    DY, DX, DZ0, DZ1 = range(4)
    tie = lax.optimization_barrier

    tok_pair = swap_pair(pick(tokens, 1 - half))
    tok_own = pick(tokens, half)
    cot_own = pick(cotangent, half)
    tok_core = swap_core(tok_own)
    taps_own = lax.dynamic_slice_in_dim(conv_weight, core * middle, middle, 2).astype(F32)
    taps_own = taps_own.reshape(3 * taps, pairs, LANES).transpose(1, 0, 2)
    taps_own = jnp.pad(taps_own, ((0, 0), (0, 16 - 3 * taps), (0, 0)))

    def norm_project(block):
        return project(scalars, block, gain_attn, bias_attn, qkv_weight)

    first = norm_project(tok_own)
    prepared = (cot_own, pick(cotangent, 1 - half), taps_own, gain_ffn, bias_ffn, up_bias_f, down_bias_f)
    tok_core, prepared = tie((tok_core, prepared))
    cot_own, cot_send, taps_own, gain_ffn, bias_ffn, up_bias_f, down_bias_f = prepared
    second = norm_project(tok_core)
    tok_pair, first, second = tie((tok_pair, first, second))
    tok_cross = swap_core(tok_pair)
    third = norm_project(tok_pair)
    tok_cross, third = tie((tok_cross, third))
    fourth = norm_project(tok_cross)
    cot_send, fourth = tie((cot_send, fourth))
    cot_pair = swap_pair(cot_send)
    normed, proj = zip(first, second, third, fourth)
    mixed, heads_own, heads_send, lse = attend(scalars, proj, taps_own)
    heads_recv = swap_core(heads_send)

    if fast:
        (
            residual,
            normed_ffn,
            grad_ffn,
            relu,
            result_all,
            result_give,
            sums_down,
            down_keep,
            down_send,
        ) = ffn_forward(
            scalars,
            heads_own,
            heads_recv,
            out_weight,
            (tok_own, tok_pair),
            (cot_own, cot_pair),
            gain_ffn,
            bias_ffn,
            up_weight,
            up_bias_f,
            down_weight,
            down_bias_f,
        )
        (
            grad_residual,
            grad_own,
            grad_send,
            early,
            up_keep,
            up_send,
        ) = ffn_backward(
            scalars,
            grad_ffn,
            normed_ffn,
            residual,
            heads_own,
            heads_recv,
            out_weight,
            gain_ffn,
            sums_down,
            relu,
            up_weight,
            down_weight,
        )
    else:
        row = jnp.arange(rows, dtype=jnp.int32)
        row_pos = [member * rows + row, jnp.bitwise_xor(member, 2) * rows + row]
        heads_all = jnp.concatenate(
            [
                jnp.where(core == 0, heads_own, heads_recv),
                jnp.where(core == 0, heads_recv, heads_own),
            ],
            axis=1,
        )
        (
            result,
            grad_residual,
            grad_heads,
            sums_ffn,
            sums_up,
            sums_down,
            grad_up,
            grad_down,
            grad_out,
        ) = ffn_plain(
            heads_all,
            jnp.concatenate([tok_own, tok_pair], axis=0),
            jnp.concatenate([cot_own, cot_pair], axis=0),
            (jnp.concatenate(row_pos) < length)[:, None],
            out_weight,
            gain_ffn,
            bias_ffn,
            up_weight,
            up_bias_f,
            down_weight,
            down_bias_f,
        )
        result_all, result_give = jnp.stack([result[:rows]] * 2), result[rows:]
        early = [sums_up.reshape(ff // width, width), sums_ffn, sums_down[None]]
        early = jnp.concatenate(early + [jnp.zeros((1, width), F32)], axis=0)
        grad_own = lax.dynamic_slice_in_dim(grad_heads, core * middle, middle, 1)
        grad_send = lax.dynamic_slice_in_dim(grad_heads, (1 - core) * middle, middle, 1)
    result_back = swap_pair(result_give)
    if fast:
        down_recv = swap_core(down_send)
        grad_own, grad_send, up_keep, up_send, down_recv, result_back = tie(
            (grad_own, grad_send, up_keep, up_send, down_recv, result_back)
        )
        up_recv = swap_core(up_send)
    grad_recv = swap_core(grad_send)
    if fast:
        down_rows = down_keep.shape[4]
        up_rows = up_keep.shape[4]
        each = (down_rows + up_rows) // 3
        down = (down_keep, down_recv)
        up = (up_keep, up_recv)
        rest = down_rows - each
        down_a, down_b = Segment(down, 0, each), Segment(down, each, rest)
        up_a, up_b = Segment(up, 0, each - rest), Segment(up, each - rest, each)
        group_1, group_2, group_3 = [down_a], [down_b, up_a], [up_b]

        def stage(dims, groups=(group_1, group_2, group_3)):
            return outgoing(scalars, groups, dims)

        def arrive(dims, sent, groups=(group_1, group_2, group_3)):
            for group, dim, value in zip(groups, dims, sent):
                settle(group, dim, value)

        dims = (DX, DZ0, DY)
        sent = stage(dims)
        grad_own, grad_recv, sent = tie((grad_own, grad_recv, sent))
        sent = [hop(v, hops[d]) for v, d in zip(sent, dims)]
        arrive(dims, sent)

    def backward(pair, grad_recv):
        own, send, conv, keep, give = attend_back(
            pair,
            scalars,
            proj,
            mixed,
            lse,
            taps_own,
            heads_own,
            heads_send,
            grad_own,
            grad_recv,
            normed,
        )
        keep = keep.reshape((1, 1) + keep.shape)
        give = give.reshape((1, 1) + give.shape)
        return own, send, conv, keep, give

    qkv_rows = 3 * width // 8
    own_0, send_0, conv_0, keep_0, give_0 = backward(0, grad_recv)
    if fast:
        dims = (DY, DZ1, DX)
        sent = stage(dims)
        grad_recv, own_0, send_0, give_0, sent = tie((grad_recv, own_0, send_0, give_0, sent))
        sent = [hop(v, hops[d]) for v, d in zip(sent, dims)]
        arrive(dims, sent)
        qkv_0 = Segment((keep_0, hop(give_0, hops[DX])), 0, qkv_rows)
        group_1.append(qkv_0)
    recv_0 = swap_core(send_0)
    own_1, send_1, conv_1, keep_1, give_1 = backward(1, grad_recv)
    if fast:
        dims = (DZ0, DX, DZ1)
        sent = stage(dims)
        grad_recv, own_1, send_1, give_1, recv_0, sent = tie(
            (grad_recv, own_1, send_1, give_1, recv_0, sent)
        )
        sent = [hop(v, hops[d]) for v, d in zip(sent, dims)]
        give_1 = hop(give_1, hops[DX])
    recv_1 = swap_core(send_1)
    own_2, send_2, conv_2, keep_2, give_2 = backward(2, grad_recv)
    if fast:
        own_2, send_2, give_2, recv_1, sent, give_1 = tie(
            (own_2, send_2, give_2, recv_1, sent, give_1)
        )
        arrive(dims, sent)
        qkv_1 = Segment((keep_1, give_1), 0, qkv_rows)
        give_2 = hop(give_2, hops[DX])
    recv_2 = swap_core(send_2)
    if fast:
        dims = (DZ1, DY, DZ0)
        sent = stage(dims)
        recv_2, sent = tie((recv_2, sent))
        ffn_waiting = [hop(v, hops[d]) for v, d in zip(sent, dims)]
    g_own = (own_0, own_1, own_2)
    g_send = (send_0, send_1, send_2)
    g_recv = (recv_0, recv_1, recv_2)
    g_conv = (conv_0, conv_1, conv_2)
    grad_in_pair, sums_pair = input_grad(
        1, scalars, g_own, g_recv, qkv_weight, tok_pair, grad_residual, gain_attn
    )
    grad_in_back = swap_pair(grad_in_pair)
    tok_last = tok_own
    if fast:
        give_2, sums_pair = tie((give_2, sums_pair))
        qkv_2 = Segment((keep_2, give_2), 0, qkv_rows)
        (sent,) = outgoing(scalars, [[qkv_1, qkv_2]], [DZ0])
        tok_last, sums_pair, sent = tie((tok_own, sums_pair, sent))
        waiting = hop(sent, hops[DZ0])
    tokens_grad, small = input_grad(
        0,
        scalars,
        g_own,
        g_recv,
        qkv_weight,
        tok_last,
        grad_residual,
        gain_attn,
        (early, sums_pair) + g_conv,
    )

    def place(both, other):
        return lax.dynamic_update_slice(both, other[None], (1 - half, 0, 0))

    result_all = place(result_all, result_back)
    index = batch * groups + member
    share = width // devices
    part = width // batch_groups

    if not fast:
        axes = ("batch", "mp")
        grad_qkv = 0.0
        for n, (norm, slot) in enumerate(zip(normed, (0, 0, 1, 1))):
            source = (g_own, g_send)[n % 2]
            grads = jnp.concatenate([g[slot * rows : (slot + 1) * rows] for g in source], axis=1)
            grad_qkv = grad_qkv + jnp.einsum("dt,te->de", norm, grads, preferred_element_type=F32)
        grad_qkv = grad_qkv.reshape(width, pairs, 3, LANES).transpose(2, 0, 1, 3)
        qkv_full = lax.dynamic_update_slice_in_dim(
            jnp.zeros((3, width, width), F32), grad_qkv.reshape(3, width, middle), core * middle, 2
        )
        qkv_flat = qkv_full.reshape(3, batch_groups, part, groups, quarter)
        qkv_flat = qkv_flat.transpose(1, 3, 0, 2, 4).reshape(devices * 3 * part, quarter)

        def scatter(value):
            return lax.psum_scatter(value, axes, scatter_dimension=0, tiled=True)

        small = lax.psum(small, axes)
        qkv_out = scatter(qkv_flat).reshape(3, part, quarter)
        up_out, down_out, out_out = scatter(grad_up), scatter(grad_down), scatter(grad_out)
    else:
        small = small + hop(small, ("mp", CORE))
        small, waiting = tie((small, waiting))
        settle([qkv_1, qkv_2], DZ0, waiting)
        (sent,) = outgoing(scalars, [[qkv_1, qkv_2]], [DZ1])
        sent = hop(sent, hops[DZ1])
        small = small + hop(small, hops[DX])
        small, ffn_waiting = tie((small, ffn_waiting))
        arrive((DZ1, DY, DZ0), ffn_waiting)
        small = small + hop(small, hops[DZ0])
        small, sent, grad_in_back = tie((small, sent, grad_in_back))
        settle([qkv_1, qkv_2], DZ1, sent)
        small = small + hop(small, hops[DZ1])
        small = small + hop(small, hops[DY])

        def finish_ffn(s_ref, totals, outs):
            whole = [total((0,) * 4, slice(None)) for total in totals]
            downs = jnp.concatenate(whole[0:2], axis=0)
            ups = jnp.concatenate(whole[2:4], axis=0)
            down_out, up_out, out_out = outs
            for out, values in ((down_out, downs), (up_out, ups), (out_out, ups[down_rows:])):
                size, cols = out.shape
                for n in range(cols // LANES):
                    out[:, n * LANES : (n + 1) * LANES] = values[n * size : (n + 1) * size]

        down_out, up_out, out_out = sum_call(
            scalars,
            [down_a, down_b, up_a, up_b],
            [None] * 4,
            finish_ffn,
            [
                jax.ShapeDtypeStruct((ff // devices, width), F32),
                jax.ShapeDtypeStruct((share, ff), F32),
                jax.ShapeDtypeStruct((share, width), F32),
            ],
            "ffn_sum",
        )

        def finish_qkv(s_ref, totals, outs):
            first, middle, last = [total((0,) * 4, slice(None)) for total in totals]
            lower = jnp.concatenate([first, middle[:, :HEAD_DIM]], axis=1)
            upper = jnp.concatenate([middle[:, HEAD_DIM:], last], axis=1)
            outs[0][...] = jnp.where(s_ref[0] == 0, lower, upper)
            outs[1][...] = jnp.where(s_ref[4] == 0, upper, lower).astype(BF16)
            outs[2][...] = jnp.where(s_ref[4] == 0, lower, upper).astype(BF16)

        keep, straight, crossed = sum_call(
            scalars,
            [qkv_0, qkv_1, qkv_2],
            [None] * 3,
            finish_qkv,
            [jax.ShapeDtypeStruct((qkv_rows, quarter), t) for t in (F32, BF16, BF16)],
            "qkv_sum",
        )
        straight = lax.ppermute(straight, "mp", [(2, 0), (0, 1), (3, 2), (1, 3)])
        crossed = lax.ppermute(crossed, "mp", [(2, 1), (1, 2)])
        qkv_out = straight.astype(F32) + jnp.where(half == core, keep, crossed.astype(F32))
        qkv_out = qkv_out.reshape(3, part, quarter)

    tokens_grad = place(tokens_grad, grad_in_back)
    up_bias_out = pick(small[: ff // width].reshape(devices, ff // devices), index)
    mine = pick(small.reshape(24, devices, share).transpose(1, 0, 2), index)
    return (
        result_all,
        tokens_grad,
        mine[17],
        mine[18],
        qkv_out,
        mine[8:17].reshape(3, taps, share),
        out_out,
        mine[4],
        mine[5],
        up_out,
        up_bias_out,
        down_out,
        mine[6],
    )


def solution(mesh):
    in_specs = (
        P("batch", "mp", None),
        P("batch", "mp", None),
        P("batch"),
    ) + (P(),) * 11
    out_specs = (
        P("batch", "mp", None),
        P("batch", "mp", None),
        P(("batch", "mp")),
        P(("batch", "mp")),
        P(None, "batch", "mp"),
        P(None, None, ("batch", "mp")),
        P(("batch", "mp"), None),
        P(("batch", "mp")),
        P(("batch", "mp")),
        P(("batch", "mp"), None),
        P(("batch", "mp")),
        P(("batch", "mp"), None),
        P(("batch", "mp")),
    )
    return jax.shard_map(
        on_device, mesh=mesh, in_specs=in_specs, out_specs=out_specs, check_vma=False
    )
```

profile of v0, /device:TPU:0, one launch (start us, length us, event | category | flops | bytes accessed | tf_op | source)
XLA Modules:
  0.0 287.7 jit_solution(3367615678705388390)
XLA Ops:
  11.6 5.3 %project.4 = (bf16[768,512]{1,0:T(8,128)(2,1)}, bf16[512,1152]{1,0:T(8,128)(2,1)}) custom-call(s32[7]{0:T(128)} %stack.27.s_ref.m_ref, bf16[512,768]{1,0:T(8,128)(2,1)} %copy-done.4, f32[1,768]{1,0:T(1,128)} %reshape.131.gain_ref, f32[1,768]{1,0:T(1,128)} %reshape.133.bias_ref, bf16[3,768,768]{2,1,0:T(8,128)(2,1)} %w_ref.11), custom_call_target="tpu_custom_call" | custom-call | flops 1048576 | bytes 65536 | tf_op jit(solution)/shard_map/project/pallas_call | solution.py:85
  17.5 2.6 dynamic-slice_bitcast_fusion
  20.2 5.3 %project.5 = (bf16[768,512]{1,0:T(8,128)(2,1)}, bf16[512,1152]{1,0:T(8,128)(2,1)}) custom-call(s32[7]{0:T(128)} %stack.27.s_ref.m_ref, bf16[512,768]{1,0:T(8,128)(2,1)} %collective-permute-done.1.x_ref, f32[1,768]{1,0:T(1,128)} %reshape.131.gain_ref, f32[1,768]{1,0:T(1,128)} %reshape.133.bias_ref, bf16[3,768,768]{2,1,0:T(8,128)(2,1)} %w_ref.11), custom_call_target="tpu_custom_call" | custom-call | flops 1048576 | bytes 65536 | tf_op jit(solution)/shard_map/project/pallas_call | solution.py:85
  26.4 5.3 %project.6 = (bf16[768,512]{1,0:T(8,128)(2,1)}, bf16[512,1152]{1,0:T(8,128)(2,1)}) custom-call(s32[7]{0:T(128)} %stack.27.s_ref.m_ref, bf16[512,768]{1,0:T(8,128)(2,1)} %copy-done.6, f32[1,768]{1,0:T(1,128)} %reshape.131.gain_ref, f32[1,768]{1,0:T(1,128)} %reshape.133.bias_ref, bf16[3,768,768]{2,1,0:T(8,128)(2,1)} %w_ref.11), custom_call_target="tpu_custom_call" | custom-call | flops 1048576 | bytes 65536 | tf_op jit(solution)/shard_map/project/pallas_call | solution.py:85
  32.6 5.4 %project.7 = (bf16[768,512]{1,0:T(8,128)(2,1)}, bf16[512,1152]{1,0:T(8,128)(2,1)}) custom-call(s32[7]{0:T(128)} %stack.27.s_ref.m_ref, bf16[512,768]{1,0:T(8,128)(2,1)} %copy-done.20, f32[1,768]{1,0:T(1,128)} %reshape.131.gain_ref, f32[1,768]{1,0:T(1,128)} %reshape.133.bias_ref, bf16[3,768,768]{2,1,0:T(8,128)(2,1)} %w_ref.11), custom_call_target="tpu_custom_call" | custom-call | flops 1048576 | bytes 65536 | tf_op jit(solution)/shard_map/project/pallas_call | solution.py:85
  38.7 26.3 %attend.1 = (bf16[2048,1152]{1,0:T(8,128)(2,1)}, bf16[1024,384]{1,0:T(8,128)(2,1)}, bf16[1024,384]{1,0:T(8,128)(2,1)}, f32[3,2,2048]{2,1,0:T(2,128)}) custom-call(s32[7]{0:T(128)} %stack.27.s_ref.m_ref, bf16[512,1152]{1,0:T(8,128)(2,1)} %get-tuple-element.153.p0, bf16[512,1152]{1,0:T(8,128)(2,1)} %get-tuple-element.154.p1, ...), custom_call_target="tpu_custom_call" | custom-call | flops 1048576 | bytes 65536 | tf_op jit(solution)/shard_map/attend/pallas_call | solution.py:190
  68.5 27.7 %ffn_forward.1 = (f32[1024,768]{1,0:T(8,128)}, bf16[1024,768]{1,0:T(8,128)(2,1)}, bf16[1024,768]{1,0:T(8,128)(2,1)}, f32[1024,3072]{1,0:T(8,128)}, bf16[2,512,76...) custom-call(s32[7]{0:T(128)} %stack.27.s_ref.m_ref, ...), custom_call_target="tpu_custom_call" | custom-call | flops 1048576 | bytes 65536 | tf_op jit(solution)/shard_map/ffn_forward/pallas_call | solution.py:492
  97.7 29.7 %ffn_backward.1 = (f32[1024,768]{1,0:T(8,128)}, bf16[1024,384]{1,0:T(8,128)(2,1)}, bf16[1024,384]{1,0:T(8,128)(2,1)}, f32[8,768]{1,0:T(8,128)}, bf16[2,2,2,2,720...) custom-call(s32[7]{0:T(128)} %stack.27.s_ref.m_ref, bf16[1024,768]{1,0:T(8,128)(2,1)} %get-tuple-element.174.gf_ref, ...), custom_call_target="tpu_custom_call" | custom-call | flops 1048576 | bytes 65536 | tf_op jit(solution)/shard_map/ffn_backward/pallas_call | solution.py:621
  128.8 6.3 %collective-permute-done.8.refs_3_.refs_5_.refs_9_.refs_11_ = bf16[2,2,2,2,720,128]{5,4,3,2,1,0:T(8,128)(2,1)} collective-permute-done((bf16[2,2,2,2,720,128]{5,4,3,2,1,0:T(8,128)(2,1)}, bf16[2,2,2,2,720,128]{5,4,3,2,1,0:T(8,128)(2,1)}, u32[]{:S(2)}, u32[]{:S(2)}) %collective-permute-start.8) | collective-permute-done | bytes 2949152 | tf_op jit(solution)/shard_map/ppermute | solution.py:919
  135.2 4.9 %stage_sum.6 = (bf16[2,1,2,2,432,128]{5,4,3,2,1,0:T(8,128)(2,1)}, bf16[2,2,1,2,432,128]{5,4,3,2,1,0:T(8,128)(2,1)}, bf16[1,2,2,2,432,128]{5,4,3,2,1,0:T(8,128)(2,1)}) custom-call(s32[7]{0:T(128)} %stack.27.s_ref.m_ref, bf16[2,2,2,2,576,128]{5,4,3,2,1,0:T(8,128)(2,1)} %get-tuple-element.188.refs_0_, ...), custom_call_target="tpu_custom_call" | custom-call | flops 1048576 | bytes 65536 | tf_op jit(solution)/shard_map/stage_sum/pallas_call | solution.py:804
  144.9 19.7 %attend_back.3 = (bf16[1024,384]{1,0:T(8,128)(2,1)}, bf16[1024,384]{1,0:T(8,128)(2,1)}, f32[16,128]{1,0:T(8,128)}, bf16[2,2,288,128]{3,2,1,0:T(8,128)(2,1)}, bf16[2,2,288,128]{3,2,1,0:T(8,128)(2,1)}) custom-call(s32[7]{0:T(128)} %stack.27.s_ref.m_ref, bf16[512,1152]{1,0:T(8,128)(2,1)} %get-tuple-element.153.p0, bf16[512,1152]{1,0:T(8,128)(2,1)} %get-tuple-element.154.p1, ...), custom_call_target="tpu_custom_call" | custom-call | flops 1048576 | bytes 65536 | tf_op jit(solution)/shard_map/attend_back/pallas_call | solution.py:354
  165.8 4.1 %stage_sum.7 = (bf16[1,1,2,2,432,128]{5,4,3,2,1,0:T(8,128)(2,1)}, bf16[2,2,1,1,432,128]{5,4,3,2,1,0:T(8,128)(2,1)}, bf16[1,1,2,2,432,128]{5,4,3,2,1,0:T(8,128)(2,1)}) custom-call(s32[7]{0:T(128)} %stack.27.s_ref.m_ref, bf16[2,2,2,2,576,128]{5,4,3,2,1,0:T(8,128)(2,1)} %get-tuple-element.188.refs_0_, ...), custom_call_target="tpu_custom_call" | custom-call | flops 1048576 | bytes 65536 | tf_op jit(solution)/shard_map/stage_sum/pallas_call | solution.py:804
  176.0 19.7 %attend_back.4 = (bf16[1024,384]{1,0:T(8,128)(2,1)}, bf16[1024,384]{1,0:T(8,128)(2,1)}, f32[16,128]{1,0:T(8,128)}, bf16[2,2,288,128]{3,2,1,0:T(8,128)(2,1)}, bf16[2,2,288,128]{3,2,1,0:T(8,128)(2,1)}) custom-call(s32[7]{0:T(128)} %stack.27.s_ref.m_ref, bf16[512,1152]{1,0:T(8,128)(2,1)} %get-tuple-element.153.p0, bf16[512,1152]{1,0:T(8,128)(2,1)} %get-tuple-element.154.p1, ...), custom_call_target="tpu_custom_call" | custom-call | flops 1048576 | bytes 65536 | tf_op jit(solution)/shard_map/attend_back/pallas_call | solution.py:354
  196.9 3.8 %stage_sum.8 = (bf16[1,1,1,2,720,128]{5,4,3,2,1,0:T(8,128)(2,1)}, bf16[2,1,1,1,432,128]{5,4,3,2,1,0:T(8,128)(2,1)}, bf16[1,1,2,1,432,128]{5,4,3,2,1,0:T(8,128)(2,1)}) custom-call(s32[7]{0:T(128)} %stack.27.s_ref.m_ref, bf16[2,2,2,2,576,128]{5,4,3,2,1,0:T(8,128)(2,1)} %get-tuple-element.188.refs_0_, ...), custom_call_target="tpu_custom_call" | custom-call | flops 1048576 | bytes 65536 | tf_op jit(solution)/shard_map/stage_sum/pallas_call | solution.py:804
  204.2 19.9 %attend_back.5 = (bf16[1024,384]{1,0:T(8,128)(2,1)}, bf16[1024,384]{1,0:T(8,128)(2,1)}, f32[16,128]{1,0:T(8,128)}, bf16[2,2,288,128]{3,2,1,0:T(8,128)(2,1)}, bf16[2,2,288,128]{3,2,1,0:T(8,128)(2,1)}) custom-call(s32[7]{0:T(128)} %stack.27.s_ref.m_ref, bf16[512,1152]{1,0:T(8,128)(2,1)} %get-tuple-element.153.p0, bf16[512,1152]{1,0:T(8,128)(2,1)} %get-tuple-element.154.p1, ...), custom_call_target="tpu_custom_call" | custom-call | flops 1048576 | bytes 65536 | tf_op jit(solution)/shard_map/attend_back/pallas_call | solution.py:354
  225.5 3.3 %stage_sum.9 = (bf16[1,1,1,1,720,128]{5,4,3,2,1,0:T(8,128)(2,1)}, bf16[1,1,1,1,432,128]{5,4,3,2,1,0:T(8,128)(2,1)}, bf16[1,1,1,1,432,128]{5,4,3,2,1,0:T(8,128)(2,1)}) custom-call(s32[7]{0:T(128)} %stack.27.s_ref.m_ref, bf16[2,2,2,2,576,128]{5,4,3,2,1,0:T(8,128)(2,1)} %get-tuple-element.188.refs_0_, ...), custom_call_target="tpu_custom_call" | custom-call | flops 1048576 | bytes 65536 | tf_op jit(solution)/shard_map/stage_sum/pallas_call | solution.py:804
  229.7 7.8 %input_grad.2 = (bf16[512,768]{1,0:T(8,128)(2,1)}, f32[8,768]{1,0:T(8,128)}) custom-call(s32[7]{0:T(128)} %stack.27.s_ref.m_ref, bf16[1024,384]{1,0:T(8,128)(2,1)} %get-tuple-element.212.o0, bf16[1024,384]{1,0:T(8,128)(2,1)} %get-tuple-element.226.o1, bf16[1024,384]{1,0:T(8,128)(2,1)} %get-tuple-element.236.o2, ...), custom_call_target="tpu_custom_call" | custom-call | flops 1048576 | bytes 65536 | tf_op jit(solution)/shard_map/input_grad/pallas_call | solution.py:695
  242.1 8.0 %input_grad.3 = (bf16[2,512,768]{2,1,0:T(8,128)(2,1)}, f32[24,768]{1,0:T(8,128)}) custom-call(s32[7]{0:T(128)} %stack.27.s_ref.m_ref, bf16[1024,384]{1,0:T(8,128)(2,1)} %get-tuple-element.212.o0, bf16[1024,384]{1,0:T(8,128)(2,1)} %get-tuple-element.226.o1, bf16[1024,384]{1,0:T(8,128)(2,1)} %get-tuple-element.236.o2, ...), custom_call_target="tpu_custom_call" | custom-call | flops 1048576 | bytes 65536 | tf_op jit(solution)/shard_map/input_grad/pallas_call | solution.py:695
  250.2 2.6 collective-permute-start.27
  262.5 2.8 collective-permute-start.30
  266.2 3.4 %ffn_sum.1 = (f32[96,768]{1,0:T(8,128)}, f32[24,3072]{1,0:T(8,128)}, f32[24,768]{1,0:T(8,128)}) custom-call(s32[7]{0:T(128)} %stack.27.s_ref.m_ref, bf16[2,2,2,2,576,128]{5,4,3,2,1,0:T(8,128)(2,1)} %get-tuple-element.188.refs_0_, bf16[2,2,2,2,576,128]{5,4,3,2,1,0:T(8,128)(2,1)} %collective-permute-done.5.refs_1_, bf16[2,1,2,2,432,128]{5,4,3,2,1,0:T(8,128)(2,1)} %copy-done.2, ...), custom_call_target="tpu_custom_call" | custom-call | flops 1048576 | bytes 65536 | tf_op jit(solution)/shard_map/ffn_sum/pallas_call | solution.py:804
  269.7 4.4 %collective-permute-start.33 = (f32[24,768]{1,0:T(8,128)S(1)}, f32[24,768]{1,0:T(8,128)S(1)}, u32[]{:S(2)}, u32[]{:S(2)}) collective-permute-start(f32[24,768]{1,0:T(8,128)S(1)} %add.47), channel_id=1, source_target_pairs={{0,16},{4,20},{8,24},{12,28},{16,0},{20,4},{24,8},{28,12},{1,17},{... | collective-permute-start | bytes 221192 | tf_op jit(solution)/shard_map/ppermute | solution.py:844
  274.1 3.0 %qkv_sum.1 = (f32[288,192]{1,0:T(8,128)}, bf16[288,192]{1,0:T(8,128)(2,1)}, bf16[288,192]{1,0:T(8,128)(2,1)}) custom-call(s32[7]{0:T(128)} %stack.27.s_ref.m_ref, bf16[1,1,2,2,288,128]{5,4,3,2,1,0:T(8,128)(2,1)} %bitcast.50, bf16[1,1,2,2,288,128]{5,4,3,2,1,0:T(8,128)(2,1)} %copy-done.15, bf16[1,1,1,2,720,128]{5,4,3,2,1,0:T(8,128)(2,1)} %copy-done.10, ...), custom_call_target="tpu_custom_call" | custom-call | flops 1048576 | bytes 65536 | tf_op jit(solution)/shard_map/qkv_sum/pallas_call | solution.py:804
  278.9 3.2 %collective-permute-start.34 = (f32[24,768]{1,0:T(8,128)S(1)}, f32[24,768]{1,0:T(8,128)S(1)}, u32[]{:S(2)}, u32[]{:S(2)}) collective-permute-start(f32[24,768]{1,0:T(8,128)S(1)} %add.48), channel_id=1, source_target_pairs={{0,2},{1,3},{2,0},{3,1},{4,6},{5,7},{6,4},{7,5},{8,10},{9,11},{10,... | collective-permute-start | bytes 221192 | tf_op jit(solution)/shard_map/ppermute | solution.py:844
  (164 shorter events, 61.5 us)
Async XLA Ops:
  3.1 17.1 %collective-permute-start.1 = (bf16[512,768]{1,0:T(8,128)(2,1)S(1)}, bf16[512,768]{1,0:T(8,128)(2,1)}, u32[]{:S(2)}, u32[]{:S(2)}) collective-permute-start(bf16[512,768]{1,0:T(8,128)(2,1)S(1)} %get-tuple-element.255.x_ref.tok0), channel_id=1, source_target_pairs={{0,1},{1,0},{2,3},{3,2},{4,5},{5,4},{6,7},{7,6},{8,9},{9,8},{10,11... | collective-permute-start | bytes 2359304 | tf_op jit(solution)/shard_map/ppermute | solution.py:919
  3.6 21.9 %collective-permute-start = (bf16[512,768]{1,0:T(8,128)(2,1)}, bf16[512,768]{1,0:T(8,128)(2,1)S(1)}, u32[]{:S(2)}, u32[]{:S(2)}) collective-permute-start(bf16[512,768]{1,0:T(8,128)(2,1)} %get-tuple-element.286), channel_id=1, source_target_pairs={{0,2},{1,3},{2,0},{3,1},{4,6},{5,7},{6,4},{7,5},{8,10},{9,11},{10,... | collective-permute-start | bytes 2359304 | tf_op jit(solution)/shard_map/ppermute | solution.py:922
  38.0 27.1 %collective-permute-start.4 = (bf16[512,768]{1,0:T(8,128)(2,1)}, bf16[512,768]{1,0:T(8,128)(2,1)S(1)}, u32[]{:S(2)}, u32[]{:S(2)}) collective-permute-start(bf16[512,768]{1,0:T(8,128)(2,1)} %get-tuple-element.168), channel_id=1, source_target_pairs={{0,2},{1,3},{2,0},{3,1},{4,6},{5,7},{6,4},{7,5},{8,10},{9,11},{10,... | collective-permute-start | bytes 2359304 | tf_op jit(solution)/shard_map/ppermute | solution.py:922
  96.2 31.2 %collective-permute-start.5 = (bf16[2,2,2,2,576,128]{5,4,3,2,1,0:T(8,128)(2,1)}, bf16[2,2,2,2,576,128]{5,4,3,2,1,0:T(8,128)(2,1)}, u32[]{:S(2)}, u32[]{:S(2)}) collective-permute-start(bf16[2,2,2,2,576,128]{5,4,3,2,1,0:T(8,128)(2,1)} %get-tuple-element.183), channel_id=1, source_target_pairs={{0,1},{1,0},{2,3},{3,2},{4,5},{5,4},{6,7},{7,6},{8,9},{9,8},{10,11... | collective-permute-start | bytes 7077896 | tf_op jit(solution)/shard_map/ppermute | solution.py:919
  96.4 31.0 %collective-permute-start.6 = (bf16[512,768]{1,0:T(8,128)(2,1)}, bf16[512,768]{1,0:T(8,128)(2,1)S(1)}, u32[]{:S(2)}, u32[]{:S(2)}) collective-permute-start(bf16[512,768]{1,0:T(8,128)(2,1)} %get-tuple-element.184), channel_id=1, source_target_pairs={{0,2},{1,3},{2,0},{3,1},{4,6},{5,7},{6,4},{7,5},{8,10},{9,11},{10,... | collective-permute-start | bytes 2359304 | tf_op jit(solution)/shard_map/ppermute | solution.py:922
  128.4 11.7 %collective-permute-start.7 = (bf16[1024,384]{1,0:T(8,128)(2,1)}, bf16[1024,384]{1,0:T(8,128)(2,1)S(1)}, u32[]{:S(2)}, u32[]{:S(2)}) collective-permute-start(bf16[1024,384]{1,0:T(8,128)(2,1)} %get-tuple-element.187), channel_id=1, source_target_pairs={{0,1},{1,0},{2,3},{3,2},{4,5},{5,4},{6,7},{7,6},{8,9},{9,8},{10,11... | collective-permute-start | bytes 2359304 | tf_op jit(solution)/shard_map/ppermute | solution.py:919
  141.1 23.5 %collective-permute-start.9 = (bf16[2,1,2,2,432,128]{5,4,3,2,1,0:T(8,128)(2,1)}, bf16[2,1,2,2,432,128]{5,4,3,2,1,0:T(8,128)(2,1)S(1)}, u32[]{:S(2)}, u32[]{:S(2)}) collective-permute-start(bf16[2,1,2,2,432,128]{5,4,3,2,1,0:T(8,128)(2,1)} %get-tuple-element.206), channel_id=1, source_target_pairs={{0,4},{4,0},{8,12},{12,8},{16,20},{20,16},{24,28},{28,24},{1,5},{5... | collective-permute-start | bytes 2654216 | tf_op jit(solution)/shard_map/ppermute | solution.py:844
  142.6 22.0 %collective-permute-start.10 = (bf16[2,2,1,2,432,128]{5,4,3,2,1,0:T(8,128)(2,1)}, bf16[2,2,1,2,432,128]{5,4,3,2,1,0:T(8,128)(2,1)S(1)}, u32[]{:S(2)}, u32[]{:S(2)}) collective-permute-start(bf16[2,2,1,2,432,128]{5,4,3,2,1,0:T(8,128)(2,1)} %get-tuple-element.207), channel_id=1, source_target_pairs={{0,8},{4,12},{8,0},{12,4},{16,24},{20,28},{24,16},{28,20},{1,9},{5... | collective-permute-start | bytes 2654216 | tf_op jit(solution)/shard_map/ppermute | solution.py:844
  144.2 21.4 %collective-permute-start.11 = (bf16[1,2,2,2,432,128]{5,4,3,2,1,0:T(8,128)(2,1)}, bf16[1,2,2,2,432,128]{5,4,3,2,1,0:T(8,128)(2,1)}, u32[]{:S(2)}, u32[]{:S(2)}) collective-permute-start(bf16[1,2,2,2,432,128]{5,4,3,2,1,0:T(8,128)(2,1)} %get-tuple-element.208), channel_id=1, source_target_pairs={{0,2},{1,3},{2,0},{3,1},{4,6},{5,7},{6,4},{7,5},{8,10},{9,11},{10,... | collective-permute-start | bytes 2654216 | tf_op jit(solution)/shard_map/ppermute | solution.py:844
  170.0 30.7 %collective-permute-start.12 = (bf16[1024,384]{1,0:T(8,128)(2,1)}, bf16[1024,384]{1,0:T(8,128)(2,1)}, u32[]{:S(2)}, u32[]{:S(2)}) collective-permute-start(bf16[1024,384]{1,0:T(8,128)(2,1)} %get-tuple-element.217), channel_id=1, source_target_pairs={{0,1},{1,0},{2,3},{3,2},{4,5},{5,4},{6,7},{7,6},{8,9},{9,8},{10,11... | collective-permute-start | bytes 2359304 | tf_op jit(solution)/shard_map/ppermute | solution.py:919
  170.0 25.7 %collective-permute-start.13 = (bf16[1,1,2,2,432,128]{5,4,3,2,1,0:T(8,128)(2,1)}, bf16[1,1,2,2,432,128]{5,4,3,2,1,0:T(8,128)(2,1)S(1)}, u32[]{:S(2)}, u32[]{:S(2)}) collective-permute-start(bf16[1,1,2,2,432,128]{5,4,3,2,1,0:T(8,128)(2,1)} %get-tuple-element.218), channel_id=1, source_target_pairs={{0,2},{1,3},{2,0},{3,1},{4,6},{5,7},{6,4},{7,5},{8,10},{9,11},{10,... | collective-permute-start | bytes 1327112 | tf_op jit(solution)/shard_map/ppermute | solution.py:844
  171.4 24.3 %collective-permute-start.15 = (bf16[2,2,1,1,432,128]{5,4,3,2,1,0:T(8,128)(2,1)}, bf16[2,2,1,1,432,128]{5,4,3,2,1,0:T(8,128)(2,1)S(1)}, u32[]{:S(2)}, u32[]{:S(2)}) collective-permute-start(bf16[2,2,1,1,432,128]{5,4,3,2,1,0:T(8,128)(2,1)} %get-tuple-element.221), channel_id=1, source_target_pairs={{0,16},{4,20},{8,24},{12,28},{16,0},{20,4},{24,8},{28,12},{1,17},{... | collective-permute-start | bytes 1327112 | tf_op jit(solution)/shard_map/ppermute | solution.py:844
  174.0 21.8 %collective-permute-start.16 = (bf16[1,1,2,2,432,128]{5,4,3,2,1,0:T(8,128)(2,1)}, bf16[1,1,2,2,432,128]{5,4,3,2,1,0:T(8,128)(2,1)S(1)}, u32[]{:S(2)}, u32[]{:S(2)}) collective-permute-start(bf16[1,1,2,2,432,128]{5,4,3,2,1,0:T(8,128)(2,1)} %get-tuple-element.222), channel_id=1, source_target_pairs={{0,4},{4,0},{8,12},{12,8},{16,20},{20,16},{24,28},{28,24},{1,5},{5... | collective-permute-start | bytes 1327112 | tf_op jit(solution)/shard_map/ppermute | solution.py:844
  174.5 21.2 %collective-permute-start.14 = (bf16[1,1,2,2,288,128]{5,4,3,2,1,0:T(8,128)(2,1)}, bf16[1,1,2,2,288,128]{5,4,3,2,1,0:T(8,128)(2,1)S(1)}, u32[]{:S(2)}, u32[]{:S(2)}) collective-permute-start(bf16[1,1,2,2,288,128]{5,4,3,2,1,0:T(8,128)(2,1)} %bitcast.57), channel_id=1, source_target_pairs={{0,4},{4,0},{8,12},{12,8},{16,20},{20,16},{24,28},{28,24},{1,5},{5... | collective-permute-start | bytes 884744 | tf_op jit(solution)/shard_map/ppermute | solution.py:844
  200.7 23.5 %collective-permute-start.17 = (bf16[1024,384]{1,0:T(8,128)(2,1)}, bf16[1024,384]{1,0:T(8,128)(2,1)S(1)}, u32[]{:S(2)}, u32[]{:S(2)}) collective-permute-start(bf16[1024,384]{1,0:T(8,128)(2,1)} %get-tuple-element.231), channel_id=1, source_target_pairs={{0,1},{1,0},{2,3},{3,2},{4,5},{5,4},{6,7},{7,6},{8,9},{9,8},{10,11... | collective-permute-start | bytes 2359304 | tf_op jit(solution)/shard_map/ppermute | solution.py:919
  200.8 23.4 %collective-permute-start.18 = (bf16[1,1,1,2,720,128]{5,4,3,2,1,0:T(8,128)(2,1)}, bf16[1,1,1,2,720,128]{5,4,3,2,1,0:T(8,128)(2,1)S(1)}, u32[]{:S(2)}, u32[]{:S(2)}) collective-permute-start(bf16[1,1,1,2,720,128]{5,4,3,2,1,0:T(8,128)(2,1)} %get-tuple-element.232), channel_id=1, source_target_pairs={{0,8},{4,12},{8,0},{12,4},{16,24},{20,28},{24,16},{28,20},{1,9},{5... | collective-permute-start | bytes 1105928 | tf_op jit(solution)/shard_map/ppermute | solution.py:844
  201.3 22.8 %collective-permute-start.21 = (bf16[1,1,2,2,288,128]{5,4,3,2,1,0:T(8,128)(2,1)}, bf16[1,1,2,2,288,128]{5,4,3,2,1,0:T(8,128)(2,1)S(1)}, u32[]{:S(2)}, u32[]{:S(2)}) collective-permute-start(bf16[1,1,2,2,288,128]{5,4,3,2,1,0:T(8,128)(2,1)} %bitcast.14), channel_id=1, source_target_pairs={{0,4},{4,0},{8,12},{12,8},{16,20},{20,16},{24,28},{28,24},{1,5},{5... | collective-permute-start | bytes 884744 | tf_op jit(solution)/shard_map/ppermute | solution.py:844
  201.8 22.3 %collective-permute-start.19 = (bf16[2,1,1,1,432,128]{5,4,3,2,1,0:T(8,128)(2,1)}, bf16[2,1,1,1,432,128]{5,4,3,2,1,0:T(8,128)(2,1)S(1)}, u32[]{:S(2)}, u32[]{:S(2)}) collective-permute-start(bf16[2,1,1,1,432,128]{5,4,3,2,1,0:T(8,128)(2,1)} %get-tuple-element.233), channel_id=1, source_target_pairs={{0,4},{4,0},{8,12},{12,8},{16,20},{20,16},{24,28},{28,24},{1,5},{5... | collective-permute-start | bytes 663560 | tf_op jit(solution)/shard_map/ppermute | solution.py:844
  203.3 20.8 %collective-permute-start.20 = (bf16[1,1,2,1,432,128]{5,4,3,2,1,0:T(8,128)(2,1)}, bf16[1,1,2,1,432,128]{5,4,3,2,1,0:T(8,128)(2,1)S(1)}, u32[]{:S(2)}, u32[]{:S(2)}) collective-permute-start(bf16[1,1,2,1,432,128]{5,4,3,2,1,0:T(8,128)(2,1)} %get-tuple-element.234), channel_id=1, source_target_pairs={{0,16},{4,20},{8,24},{12,28},{16,0},{20,4},{24,8},{28,12},{1,17},{... | collective-permute-start | bytes 663560 | tf_op jit(solution)/shard_map/ppermute | solution.py:844
  225.0 13.9 %collective-permute-start.23 = (bf16[1,1,2,2,288,128]{5,4,3,2,1,0:T(8,128)(2,1)}, bf16[1,1,2,2,288,128]{5,4,3,2,1,0:T(8,128)(2,1)}, u32[]{:S(2)}, u32[]{:S(2)}) collective-permute-start(bf16[1,1,2,2,288,128]{5,4,3,2,1,0:T(8,128)(2,1)} %bitcast.56), channel_id=1, source_target_pairs={{0,4},{4,0},{8,12},{12,8},{16,20},{20,16},{24,28},{28,24},{1,5},{5... | collective-permute-start | bytes 884744 | tf_op jit(solution)/shard_map/ppermute | solution.py:844
  237.5 32.1 %collective-permute-start.32 = (bf16[512,768]{1,0:T(8,128)(2,1)}, bf16[512,768]{1,0:T(8,128)(2,1)S(1)}, u32[]{:S(2)}, u32[]{:S(2)}) collective-permute-start(bf16[512,768]{1,0:T(8,128)(2,1)} %get-tuple-element.270), channel_id=1, source_target_pairs={{0,2},{1,3},{2,0},{3,1},{4,6},{5,7},{6,4},{7,5},{8,10},{9,11},{10,... | collective-permute-start | bytes 2359304 | tf_op jit(solution)/shard_map/ppermute | solution.py:922
  241.5 14.1 %collective-permute-start.25 = (bf16[1,1,1,2,576,128]{5,4,3,2,1,0:T(8,128)(2,1)}, bf16[1,1,1,2,576,128]{5,4,3,2,1,0:T(8,128)(2,1)S(1)}, u32[]{:S(2)}, u32[]{:S(2)}) collective-permute-start(bf16[1,1,1,2,576,128]{5,4,3,2,1,0:T(8,128)(2,1)} %stage_sum.10), channel_id=1, source_target_pairs={{0,8},{4,12},{8,0},{12,4},{16,24},{20,28},{24,16},{28,20},{1,9},{5... | collective-permute-start | bytes 884744 | tf_op jit(solution)/shard_map/ppermute | solution.py:844
  250.2 12.2 %collective-permute-start.27 = (bf16[1,1,1,1,720,128]{5,4,3,2,1,0:T(8,128)(2,1)}, bf16[1,1,1,1,720,128]{5,4,3,2,1,0:T(8,128)(2,1)}, u32[]{:S(2)}, u32[]{:S(2)}) collective-permute-start(bf16[1,1,1,1,720,128]{5,4,3,2,1,0:T(8,128)(2,1)} %get-tuple-element.265), channel_id=1, source_target_pairs={{0,16},{4,20},{8,24},{12,28},{16,0},{20,4},{24,8},{28,12},{1,17},{... | collective-permute-start | bytes 552968 | tf_op jit(solution)/shard_map/ppermute | solution.py:844
  260.1 9.6 %collective-permute-start.31 = (bf16[1,1,1,1,576,128]{5,4,3,2,1,0:T(8,128)(2,1)}, bf16[1,1,1,1,576,128]{5,4,3,2,1,0:T(8,128)(2,1)S(1)}, u32[]{:S(2)}, u32[]{:S(2)}) collective-permute-start(bf16[1,1,1,1,576,128]{5,4,3,2,1,0:T(8,128)(2,1)} %stage_sum.11), channel_id=1, source_target_pairs={{0,16},{4,20},{8,24},{12,28},{16,0},{20,4},{24,8},{28,12},{1,17},{... | collective-permute-start | bytes 442376 | tf_op jit(solution)/shard_map/ppermute | solution.py:844
  (45 other events, 204.1 us)
where the time goes:
time: 293 us; the launch traced here: 288 us
  Pallas kernels  208 us (71%)
  starting transfers between devices  39.8 us (14%)
  local copies, waits for them, and re-layouts  21.1 us (7%)
  waiting for transfers between devices  13.6 us (5%)
  other arithmetic  3.8 us (1%)
    pallas_call x3, Pallas kernels, attend_back(): pl.pallas_call(attend_back_kernel, grid=(1,), in_specs=[SMEM_SPEC] + [pl....  59.2 us
    ppermute x22, starting transfers between devices, hop(): return lax.ppermute(value, stage[0], stage[1])  31.6 us
    pallas_call x1, Pallas kernels, ffn_backward(): pl.pallas_call(ffn_backward_kernel, grid=(5,), in_specs=[SMEM_SPEC] + [st...  29.7 us
    pallas_call x1, Pallas kernels, ffn_forward(): pl.pallas_call(ffn_forward_kernel, grid_spec=pltpu.PrefetchScalarGridSpec...  27.7 us
    pallas_call x8, Pallas kernels, sum_call(): pl.pallas_call(functools.partial(sum_kernel, plan, finish, len(arrays)),...  27.6 us
    pallas_call x1, Pallas kernels, attend(): pl.pallas_call(attend_kernel, grid=(pairs,), in_specs=[SMEM_SPEC] + [pl.B...  26.3 us
    pallas_call x4, Pallas kernels, project(): pl.pallas_call(project_kernel, grid_spec=pltpu.PrefetchScalarGridSpec(num...  21.3 us
    pallas_call x2, Pallas kernels, input_grad(): pl.pallas_call(functools.partial(input_grad_kernel, final), grid_spec=plt...  15.9 us
  transfers between devices with their start and end apart: 37, of which 7 were waited for; matrix products, arithmetic and copies ran while one was open for 5% of the time, Pallas kernels for 59%

commit v1 on v0

--- a/solution.py
+++ b/solution.py
@@ -109,12 +109,10 @@
 
 
 def store_parts(flag, parts, keep_ref, send_ref):
-    first = jnp.concatenate(parts[0], axis=0)
-    second = jnp.concatenate(parts[1], axis=0)
-    keep = jnp.where(flag == 0, first, second)
-    send = jnp.where(flag == 0, second, first)
-    keep_ref[...] = keep.astype(BF16).reshape(keep_ref.shape)
-    send_ref[...] = send.astype(BF16).reshape(send_ref.shape)
+    first = jnp.concatenate(parts[0], axis=0).astype(BF16)
+    second = jnp.concatenate(parts[1], axis=0).astype(BF16)
+    keep_ref[...] = jnp.where(flag == 0, first, second).reshape(keep_ref.shape)
+    send_ref[...] = jnp.where(flag == 0, second, first).reshape(send_ref.shape)
 
 
 def only_head(values, head):
@@ -402,7 +400,7 @@
     )
 
 
-def ffn_forward_kernel(
+def ffn_kernel(
     s_ref,
     hown_ref,
     hrecv_ref,
@@ -417,15 +415,21 @@
     upb_ref,
     down_ref,
     downb_ref,
-    res_ref,
-    nf_ref,
-    gf_ref,
-    relu_ref,
     out0,
     out1,
-    dbias_ref,
-    keep_ref,
-    send_ref,
+    down_keep,
+    down_send,
+    gres_ref,
+    gown_ref,
+    gsend_ref,
+    sums_ref,
+    up_keep,
+    up_send,
+    relus,
+    res,
+    nf,
+    nft,
+    gf,
     acc,
 ):
     step = pl.program_id(0)
@@ -436,124 +440,6 @@
     def valid(start):
         row = start + lax.broadcasted_iota(jnp.int32, tok0.shape, 0)
         return row < s_ref[2]
-
-    @pl.when(step == 0)
-    def _():
-        attended = dot_nn(canonical(core, hown_ref, hrecv_ref), wout_ref[...])
-        for tok, cot, (first, start) in zip((tok0, tok1), (cot0, cot1), halves):
-            rows = slice(first, first + size)
-            residual = tok[...].astype(F32) + attended[rows]
-            res_ref[rows, :] = residual
-            scaled, _ = norm_stats(residual)
-            nf_ref[rows, :] = (scaled * gain_ref[...] + bias_ref[...]).astype(BF16)
-            grad = cot[...]
-            gf_ref[rows, :] = jnp.where(valid(start), grad, jnp.zeros_like(grad))
-        dbias_ref[0:1, :] = jnp.sum(gf_ref[...].astype(F32), axis=0, keepdims=True)
-        acc[...] = jnp.zeros_like(acc)
-
-    relu = jnp.maximum(dot_nn(nf_ref[...], up_ref[...]) + upb_ref[...], 0.0)
-    relu_ref[...] = relu
-    act = (relu * relu).astype(BF16)
-    acc[...] += dot_nn(act, down_ref[...])
-    grad = dot_tn(act, gf_ref[...])
-    rows = grad.shape[0] // 8
-    store_parts(
-        core,
-        [
-            [
-                tile
-                for chunk in (bit, bit + 4, bit + 2, bit + 6)
-                for tile in lane_tiles(grad[chunk * rows : (chunk + 1) * rows])
-            ]
-            for bit in range(2)
-        ],
-        keep_ref,
-        send_ref,
-    )
-
-    @pl.when(step == pl.num_programs(0) - 1)
-    def _():
-        for out, (first, start) in zip((out0, out1), halves):
-            rows = slice(first, first + size)
-            total = res_ref[rows, :] + (acc[rows, :] + downb_ref[...])
-            out[...] = jnp.where(valid(start), total, 0.0).astype(BF16).reshape(out.shape)
-
-
-def ffn_forward(scalars, hown, hrecv, wout, toks, cots, gain, bias, up, upb, down, downb):
-    rows = 2 * toks[0].shape[0]
-    width, ff = up.shape
-    tile = ff // 4
-    part = jax.ShapeDtypeStruct((2, 2, 2, 2, tile // 8 * width // LANES, LANES), BF16)
-    part_spec = pl.BlockSpec(
-        (2, 2, 1, 1) + part.shape[4:], lambda j, _: (0, 0, lax.rem(j, 2), lax.div(j, 2), 0, 0)
-    )
-    full = lambda dtype: jax.ShapeDtypeStruct((rows, width), dtype)
-    block = jax.ShapeDtypeStruct(toks[0].shape, BF16)
-    return pl.pallas_call(
-        ffn_forward_kernel,
-        grid_spec=pltpu.PrefetchScalarGridSpec(
-            num_scalar_prefetch=1,
-            grid=(4,),
-            in_specs=[still(a) for a in (hown, hrecv, wout, *toks, *cots, gain, bias)]
-            + [
-                pl.BlockSpec((width, tile), lambda j, _: (0, j)),
-                pl.BlockSpec((1, tile), lambda j, _: (0, j)),
-                pl.BlockSpec((tile, width), lambda j, _: (j, 0)),
-                still(downb),
-            ],
-            out_specs=[once((rows, width), lambda j, _: (0, 0))] * 3
-            + [
-                pl.BlockSpec((rows, tile), lambda j, _: (0, j)),
-                once((1,) + block.shape, lambda j, s: (s[4], 0, 0)),
-                once(block.shape, lambda j, _: (0, 0)),
-                pl.BlockSpec((8, width), lambda j, _: (0, 0)),
-                part_spec,
-                part_spec,
-            ],
-            scratch_shapes=[pltpu.VMEM((rows, width), F32)],
-        ),
-        out_shape=[
-            full(F32),
-            full(BF16),
-            full(BF16),
-            jax.ShapeDtypeStruct((rows, ff), F32),
-            jax.ShapeDtypeStruct((2,) + block.shape, BF16),
-            block,
-            jax.ShapeDtypeStruct((8, width), F32),
-            part,
-            part,
-        ],
-        compiler_params=params(60),
-        cost_estimate=CHEAP,
-        name="ffn_forward",
-    )(scalars, hown, hrecv, wout, *toks, *cots, gain, bias, up, upb, down, downb)
-
-
-def ffn_backward_kernel(
-    s_ref,
-    gf_ref,
-    nf_ref,
-    res_ref,
-    hown_ref,
-    hrecv_ref,
-    wout_ref,
-    gain_ref,
-    dbias_ref,
-    relu_ref,
-    up_ref,
-    down_ref,
-    gres_ref,
-    gown_ref,
-    gsend_ref,
-    sums_ref,
-    keep_ref,
-    send_ref,
-    nft,
-    gn,
-):
-    step = pl.program_id(0)
-    last = pl.num_programs(0) - 1
-    core = s_ref[0]
 
     def store(grad):
         rows = grad.shape[0] // 32
@@ -574,32 +460,71 @@
                 ]
                 for bit in range(2)
             ],
-            keep_ref,
-            send_ref,
+            up_keep,
+            up_send,
         )
 
     @pl.when(step == 0)
     def _():
-        nft[...] = nf_ref[...].T
-        gn[...] = jnp.zeros_like(gn)
-
-    @pl.when(step < last)
+        attended = dot_nn(canonical(core, hown_ref, hrecv_ref), wout_ref[...])
+        for tok, cot, (first, start) in zip((tok0, tok1), (cot0, cot1), halves):
+            rows = slice(first, first + size)
+            residual = tok[...].astype(F32) + attended[rows]
+            res[rows, :] = residual
+            scaled, _ = norm_stats(residual)
+            nf[rows, :] = (scaled * gain_ref[...] + bias_ref[...]).astype(BF16)
+            grad = cot[...]
+            gf[rows, :] = jnp.where(valid(start), grad, jnp.zeros_like(grad))
+        sums_ref[6:7, :] = jnp.sum(gf[...].astype(F32), axis=0, keepdims=True)
+        sums_ref[7:8, :] = jnp.zeros_like(sums_ref[7:8, :])
+        acc[...] = jnp.zeros_like(acc)
+
+    @pl.when(step < 4)
     def _():
-        grad_act = dot_nt(gf_ref[...], down_ref[...])
-        grad_pre = (2.0 * relu_ref[...] * grad_act).astype(BF16)
-        sums_ref[pl.ds(step, 1), :] = jnp.sum(grad_pre.astype(F32), axis=0, keepdims=True)
-        gn[...] += dot_nt(grad_pre, up_ref[...])
+        relu = jnp.maximum(dot_nn(nf[...], up_ref[...]) + upb_ref[...], 0.0)
+        relus[step] = relu
+        act = (relu * relu).astype(BF16)
+        acc[...] += dot_nn(act, down_ref[...])
+        grad = dot_tn(act, gf[...])
+        rows = grad.shape[0] // 8
+        store_parts(
+            core,
+            [
+                [
+                    tile
+                    for chunk in (bit, bit + 4, bit + 2, bit + 6)
+                    for tile in lane_tiles(grad[chunk * rows : (chunk + 1) * rows])
+                ]
+                for bit in range(2)
+            ],
+            down_keep,
+            down_send,
+        )
+
+    @pl.when(step == 3)
+    def _():
+        for out, (first, start) in zip((out0, out1), halves):
+            rows = slice(first, first + size)
+            total = res[rows, :] + (acc[rows, :] + downb_ref[...])
+            out[...] = jnp.where(valid(start), total, 0.0).astype(BF16).reshape(out.shape)
+        nft[...] = nf[...].T
+        acc[...] = jnp.zeros_like(acc)
+
+    @pl.when((step >= 4) & (step < 8))
+    def _():
+        grad_act = dot_nt(gf[...], down_ref[...])
+        grad_pre = (2.0 * relus[step - 4] * grad_act).astype(BF16)
+        sums_ref[pl.ds(step - 4, 1), :] = jnp.sum(grad_pre.astype(F32), axis=0, keepdims=True)
+        acc[...] += dot_nt(grad_pre, up_ref[...])
         store(dot_nn(nft[...], grad_pre))
 
-    @pl.when(step == last)
+    @pl.when(step == 8)
     def _():
-        scaled, inv_std = norm_stats(res_ref[...])
-        grad = gn[...]
+        scaled, inv_std = norm_stats(res[...])
+        grad = acc[...]
         sums_ref[4:5, :] = jnp.sum(grad * scaled, axis=0, keepdims=True)
         sums_ref[5:6, :] = jnp.sum(grad, axis=0, keepdims=True)
-        sums_ref[6:7, :] = dbias_ref[0:1, :]
-        sums_ref[7:8, :] = jnp.zeros_like(sums_ref[7:8, :])
-        total = gf_ref[...].astype(F32) + norm_backward(grad, gain_ref[...], scaled, inv_std)
+        total = gf[...].astype(F32) + norm_backward(grad, gain_ref[...], scaled, inv_std)
         gres_ref[...] = total
         attended = total.astype(BF16)
         heads = dot_nt(attended, wout_ref[...]).astype(BF16)
@@ -609,45 +534,80 @@
         store(dot_tn(canonical(core, hown_ref, hrecv_ref), attended))
 
 
-def ffn_backward(scalars, gf, nf, res, hown, hrecv, wout, gain, dbias, relu, up, down):
-    rows, width = nf.shape
-    ff = up.shape[1]
+def ffn(scalars, hown, hrecv, wout, toks, cots, gain, bias, up, upb, down, downb):
+    rows = 2 * toks[0].shape[0]
+    width, ff = up.shape
     tile = ff // 4
+    assert tile == width
+    down_part = jax.ShapeDtypeStruct((2, 2, 2, 2, tile // 8 * width // LANES, LANES), BF16)
     block = width // 32 * tile // LANES
-    part = jax.ShapeDtypeStruct((2, 2, 2, 2, 5 * block, LANES), BF16)
-    part_spec = pl.BlockSpec((2, 2, 2, 2, block, LANES), lambda j: (0, 0, 0, 0, j, 0))
-    now = lambda j: jnp.minimum(j, 3)
+    up_part = jax.ShapeDtypeStruct((2, 2, 2, 2, 5 * block, LANES), BF16)
+
+    def forward(j):
+        return jnp.minimum(j, 3)
+
+    def backward(j):
+        return jnp.maximum(j - 4, 0)
+
+    def either(j):
+        return jnp.where(j < 4, j, jnp.minimum(j - 4, 3))
+
+    down_spec = pl.BlockSpec(
+        (2, 2, 1, 1) + down_part.shape[4:],
+        lambda j, _: (0, 0, lax.rem(forward(j), 2), lax.div(forward(j), 2), 0, 0),
+    )
+    up_spec = pl.BlockSpec((2, 2, 2, 2, block, LANES), lambda j, _: (0, 0, 0, 0, backward(j), 0))
+    token_block = jax.ShapeDtypeStruct(toks[0].shape, BF16)
     half = jax.ShapeDtypeStruct(hown.shape, BF16)
     return pl.pallas_call(
-        ffn_backward_kernel,
-        grid=(5,),
-        in_specs=[SMEM_SPEC]
-        + [still(a) for a in (gf, nf, res, hown, hrecv, wout, gain, dbias)]
-        + [
-            pl.BlockSpec((rows, tile), lambda j: (0, now(j))),
-            pl.BlockSpec((width, tile), lambda j: (0, now(j))),
-            pl.BlockSpec((tile, width), lambda j: (now(j), 0)),
-        ],
-        out_specs=[once((rows, width), lambda j: (0, 0))]
-        + [once(half.shape, lambda j: (0, 0))] * 2
-        + [
-            pl.BlockSpec((8, width), lambda j: (0, 0)),
-            part_spec,
-            part_spec,
-        ],
+        ffn_kernel,
+        grid_spec=pltpu.PrefetchScalarGridSpec(
+            num_scalar_prefetch=1,
+            grid=(9,),
+            in_specs=[still(a) for a in (hown, hrecv, wout, *toks, *cots, gain, bias)]
+            + [
+                pl.BlockSpec((width, tile), lambda j, _: (0, either(j))),
+                pl.BlockSpec((1, tile), lambda j, _: (0, forward(j))),
+                pl.BlockSpec((tile, width), lambda j, _: (either(j), 0)),
+                still(downb),
+            ],
+            out_specs=[
+                once((1,) + token_block.shape, lambda j, s: (s[4], 0, 0)),
+                once(token_block.shape, lambda j, _: (0, 0)),
+                down_spec,
+                down_spec,
+                once((rows, width), lambda j, _: (0, 0)),
+                once(half.shape, lambda j, _: (0, 0)),
+                once(half.shape, lambda j, _: (0, 0)),
+                pl.BlockSpec((8, width), lambda j, _: (0, 0)),
+                up_spec,
+                up_spec,
+            ],
+            scratch_shapes=[
+                pltpu.VMEM((4, rows, tile), F32),
+                pltpu.VMEM((rows, width), F32),
+                pltpu.VMEM((rows, width), BF16),
+                pltpu.VMEM((width, rows), BF16),
+                pltpu.VMEM((rows, width), BF16),
+                pltpu.VMEM((rows, width), F32),
+            ],
+        ),
         out_shape=[
+            jax.ShapeDtypeStruct((2,) + token_block.shape, BF16),
+            token_block,
+            down_part,
+            down_part,
             jax.ShapeDtypeStruct((rows, width), F32),
             half,
             half,
             jax.ShapeDtypeStruct((8, width), F32),
-            part,
-            part,
+            up_part,
+            up_part,
         ],
-        scratch_shapes=[pltpu.VMEM((width, rows), BF16), pltpu.VMEM((rows, width), F32)],
-        compiler_params=params(60),
+        compiler_params=params(63),
         cost_estimate=CHEAP,
-        name="ffn_backward",
-    )(scalars, gf, nf, res, hown, hrecv, wout, gain, dbias, relu, up, down)
+        name="ffn",
+    )(scalars, hown, hrecv, wout, *toks, *cots, gain, bias, up, upb, down, downb)
 
 
 def input_grad_kernel(
@@ -963,16 +923,17 @@
 
     if fast:
         (
-            residual,
-            normed_ffn,
-            grad_ffn,
-            relu,
             result_all,
             result_give,
-            sums_down,
             down_keep,
             down_send,
-        ) = ffn_forward(
+            grad_residual,
+            grad_own,
+            grad_send,
+            early,
+            up_keep,
+            up_send,
+        ) = ffn(
             scalars,
             heads_own,
             heads_recv,
@@ -985,27 +946,6 @@
             up_bias_f,
             down_weight,
             down_bias_f,
-        )
-        (
-            grad_residual,
-            grad_own,
-            grad_send,
-            early,
-            up_keep,
-            up_send,
-        ) = ffn_backward(
-            scalars,
-            grad_ffn,
-            normed_ffn,
-            residual,
-            heads_own,
-            heads_recv,
-            out_weight,
-            gain_ffn,
-            sums_down,
-            relu,
-            up_weight,
-            down_weight,
         )
     else:
         row = jnp.arange(rows, dtype=jnp.int32)
@@ -1045,15 +985,11 @@
         early = jnp.concatenate(early + [jnp.zeros((1, width), F32)], axis=0)
         grad_own = lax.dynamic_slice_in_dim(grad_heads, core * middle, middle, 1)
         grad_send = lax.dynamic_slice_in_dim(grad_heads, (1 - core) * middle, middle, 1)
-    result_back = swap_pair(result_give)
+    grad_recv = swap_core(grad_send)
     if fast:
         down_recv = swap_core(down_send)
-        grad_own, grad_send, up_keep, up_send, down_recv, result_back = tie(
-            (grad_own, grad_send, up_keep, up_send, down_recv, result_back)
-        )
+        grad_recv, down_recv, up_send = tie((grad_recv, down_recv, up_send))
         up_recv = swap_core(up_send)
-    grad_recv = swap_core(grad_send)
-    if fast:
         down_rows = down_keep.shape[4]
         up_rows = up_keep.shape[4]
         each = (down_rows + up_rows) // 3
@@ -1072,7 +1008,11 @@
                 settle(group, dim, value)
 
         dims = (DX, DZ0, DY)
-        sent = stage(dims)
+        sent = stage(dims[:1], (group_1,))
+        sent, grad_recv, up_recv = tie((sent, grad_recv, up_recv))
+        up_a.parts[1] = (up_recv,) + up_a.parts[1][1:]
+        up_b.parts[1] = (up_recv,) + up_b.parts[1][1:]
+        sent = list(sent) + list(stage(dims[1:], (group_2, group_3)))
         grad_own, grad_recv, sent = tie((grad_own, grad_recv, sent))
         sent = [hop(v, hops[d]) for v, d in zip(sent, dims)]
         arrive(dims, sent)
@@ -1110,19 +1050,19 @@
     if fast:
         dims = (DZ0, DX, DZ1)
         sent = stage(dims)
-        grad_recv, own_1, send_1, give_1, recv_0, sent = tie(
-            (grad_recv, own_1, send_1, give_1, recv_0, sent)
+        grad_recv, own_1, send_1, give_1, recv_0, result_give, sent = tie(
+            (grad_recv, own_1, send_1, give_1, recv_0, result_give, sent)
         )
         sent = [hop(v, hops[d]) for v, d in zip(sent, dims)]
-        give_1 = hop(give_1, hops[DX])
+    result_back = swap_pair(result_give)
     recv_1 = swap_core(send_1)
     own_2, send_2, conv_2, keep_2, give_2 = backward(2, grad_recv)
     if fast:
-        own_2, send_2, give_2, recv_1, sent, give_1 = tie(
-            (own_2, send_2, give_2, recv_1, sent, give_1)
+        own_2, send_2, give_1, give_2, recv_1, result_back, sent = tie(
+            (own_2, send_2, give_1, give_2, recv_1, result_back, sent)
         )
         arrive(dims, sent)
-        qkv_1 = Segment((keep_1, give_1), 0, qkv_rows)
+        give_1 = hop(give_1, hops[DX])
         give_2 = hop(give_2, hops[DX])
     recv_2 = swap_core(send_2)
     if fast:
@@ -1140,7 +1080,8 @@
     grad_in_back = swap_pair(grad_in_pair)
     tok_last = tok_own
     if fast:
-        give_2, sums_pair = tie((give_2, sums_pair))
+        give_1, give_2, sums_pair = tie((give_1, give_2, sums_pair))
+        qkv_1 = Segment((keep_1, give_1), 0, qkv_rows)
         qkv_2 = Segment((keep_2, give_2), 0, qkv_rows)
         (sent,) = outgoing(scalars, [[qkv_1, qkv_2]], [DZ0])
         tok_last, sums_pair, sent = tie((tok_own, sums_pair, sent))

time: 293 us -> 288 us (0.983)
  Pallas kernels: 208 us -> 203 us
    pallas_call x2 -> x1, Pallas kernels: 57.5 us -> 49.4 us  [ffn(): pl.pallas_call(ffn_kernel, grid_spec=pltpu.PrefetchScalarGridSpec(num_sca...]
    pallas_call x8 -> x9, Pallas kernels: 27.6 us -> 30.1 us  [sum_call(): pl.pallas_call(functools.partial(sum_kernel, plan, finish, len(arrays)),...]
    unnamed x64 -> x66, local copies, waits for them, and re-layouts: 7.37 us -> 4.98 us
  transfers between devices with their start and end apart: 37 -> 37, of which waited for: 7 -> 9; matrix products, arithmetic and copies ran while one was open for 5% -> 5% of each run, Pallas kernels for 59% -> 49%
where the time goes in v1:
time: 288 us; the launch traced here: 282 us
  Pallas kernels  203 us (70%)
  starting transfers between devices  39.1 us (14%)
  local copies, waits for them, and re-layouts  19.8 us (7%)
  waiting for transfers between devices  16.2 us (6%)
  other arithmetic  2.9 us (1%)
    pallas_call x3, Pallas kernels, attend_back(): pl.pallas_call(attend_back_kernel, grid=(1,), in_specs=[SMEM_SPEC] + [pl....  59.3 us
    pallas_call x1, Pallas kernels, ffn(): pl.pallas_call(ffn_kernel, grid_spec=pltpu.PrefetchScalarGridSpec(num_sca...  49.4 us
    ppermute x22, starting transfers between devices, hop(): return lax.ppermute(value, stage[0], stage[1])  30.9 us
    pallas_call x9, Pallas kernels, sum_call(): pl.pallas_call(functools.partial(sum_kernel, plan, finish, len(arrays)),...  30.1 us
    pallas_call x1, Pallas kernels, attend(): pl.pallas_call(attend_kernel, grid=(pairs,), in_specs=[SMEM_SPEC] + [pl.B...  26.5 us
    pallas_call x4, Pallas kernels, project(): pl.pallas_call(project_kernel, grid_spec=pltpu.PrefetchScalarGridSpec(num...  21.4 us
    pallas_call x2, Pallas kernels, input_grad(): pl.pallas_call(functools.partial(input_grad_kernel, final), grid_spec=plt...  16 us
    ppermute x9, waiting for transfers between devices, swap_core(): return lax.ppermute(value, 'mp', CORE)  10.4 us
  transfers between devices with their start and end apart: 37, of which 9 were waited for; matrix products, arithmetic and copies ran while one was open for 5% of the time, Pallas kernels for 49%

profile of v1, /device:TPU:0, one launch (start us, length us, event | category | flops | bytes accessed | tf_op | source)
XLA Modules:
  0.0 282.1 jit_solution(515804254550392967)
XLA Ops:
  11.5 5.3 %project.4 = (bf16[768,512]{1,0:T(8,128)(2,1)}, bf16[512,1152]{1,0:T(8,128)(2,1)}) custom-call(s32[7]{0:T(128)} %stack.27.s_ref.m_ref, bf16[512,768]{1,0:T(8,128)(2,1)} %copy-done.4, f32[1,768]{1,0:T(1,128)} %reshape.131.gain_ref, f32[1,768]{1,0:T(1,128)} %reshape.133.bias_ref, bf16[3,768,768]{2,1,0:T(8,128)(2,1)} %w_ref.11), custom_call_target="tpu_custom_call" | custom-call | flops 1048576 | bytes 65536 | tf_op jit(solution)/shard_map/project/pallas_call | solution.py:85
  17.4 2.6 dynamic-slice_bitcast_fusion
  20.1 5.3 %project.5 = (bf16[768,512]{1,0:T(8,128)(2,1)}, bf16[512,1152]{1,0:T(8,128)(2,1)}) custom-call(s32[7]{0:T(128)} %stack.27.s_ref.m_ref, bf16[512,768]{1,0:T(8,128)(2,1)} %collective-permute-done.1.x_ref, f32[1,768]{1,0:T(1,128)} %reshape.131.gain_ref, f32[1,768]{1,0:T(1,128)} %reshape.133.bias_ref, bf16[3,768,768]{2,1,0:T(8,128)(2,1)} %w_ref.11), custom_call_target="tpu_custom_call" | custom-call | flops 1048576 | bytes 65536 | tf_op jit(solution)/shard_map/project/pallas_call | solution.py:85
  26.3 5.4 %project.6 = (bf16[768,512]{1,0:T(8,128)(2,1)}, bf16[512,1152]{1,0:T(8,128)(2,1)}) custom-call(s32[7]{0:T(128)} %stack.27.s_ref.m_ref, bf16[512,768]{1,0:T(8,128)(2,1)} %copy-done.5, f32[1,768]{1,0:T(1,128)} %reshape.131.gain_ref, f32[1,768]{1,0:T(1,128)} %reshape.133.bias_ref, bf16[3,768,768]{2,1,0:T(8,128)(2,1)} %w_ref.11), custom_call_target="tpu_custom_call" | custom-call | flops 1048576 | bytes 65536 | tf_op jit(solution)/shard_map/project/pallas_call | solution.py:85
  32.5 5.4 %project.7 = (bf16[768,512]{1,0:T(8,128)(2,1)}, bf16[512,1152]{1,0:T(8,128)(2,1)}) custom-call(s32[7]{0:T(128)} %stack.27.s_ref.m_ref, bf16[512,768]{1,0:T(8,128)(2,1)} %copy-done.17, f32[1,768]{1,0:T(1,128)} %reshape.131.gain_ref, f32[1,768]{1,0:T(1,128)} %reshape.133.bias_ref, bf16[3,768,768]{2,1,0:T(8,128)(2,1)} %w_ref.11), custom_call_target="tpu_custom_call" | custom-call | flops 1048576 | bytes 65536 | tf_op jit(solution)/shard_map/project/pallas_call | solution.py:85
  38.8 26.5 %attend.1 = (bf16[2048,1152]{1,0:T(8,128)(2,1)}, bf16[1024,384]{1,0:T(8,128)(2,1)}, bf16[1024,384]{1,0:T(8,128)(2,1)}, f32[3,2,2048]{2,1,0:T(2,128)}) custom-call(s32[7]{0:T(128)} %stack.27.s_ref.m_ref, bf16[512,1152]{1,0:T(8,128)(2,1)} %get-tuple-element.150.p0, bf16[512,1152]{1,0:T(8,128)(2,1)} %get-tuple-element.151.p1, ...), custom_call_target="tpu_custom_call" | custom-call | flops 1048576 | bytes 65536 | tf_op jit(solution)/shard_map/attend/pallas_call | solution.py:188
  68.0 49.4 %ffn.1 = (bf16[2,512,768]{2,1,0:T(8,128)(2,1)}, bf16[512,768]{1,0:T(8,128)(2,1)}, bf16[2,2,2,2,576,128]{5,4,3,2,1,0:T(8,128)(2,1)}, bf16[2,2,2,2,576,128]{5,4,3,...) custom-call(s32[7]{0:T(128)} %stack.27.s_ref.m_ref, ...), custom_call_target="tpu_custom_call" | custom-call | flops 1048576 | bytes 65536 | tf_op jit(solution)/shard_map/ffn/pallas_call | solution.py:562
  117.9 5.5 %collective-permute-done.5.drecv_ref = bf16[1024,384]{1,0:T(8,128)(2,1)} collective-permute-done((bf16[1024,384]{1,0:T(8,128)(2,1)}, bf16[1024,384]{1,0:T(8,128)(2,1)}, u32[]{:S(2)}, u32[]{:S(2)}) %collective-permute-start.5) | collective-permute-done | bytes 786464 | tf_op jit(solution)/shard_map/ppermute | solution.py:879
  123.6 3.2 %stage_sum.7 = bf16[2,1,2,2,432,128]{5,4,3,2,1,0:T(8,128)(2,1)} custom-call(s32[7]{0:T(128)} %stack.27.s_ref.m_ref, bf16[2,2,2,2,576,128]{5,4,3,2,1,0:T(8,128)(2,1)} %get-tuple-element.174.refs_0_, bf16[2,2,2,2,576,128]{5,4,3,2,1,0:T(8,128)(2,1)} %collective-permute-done.6.refs_1_), custom_call_target="tpu_custom_call" | custom-call | flops 1048576 | bytes 65536 | tf_op jit(solution)/shard_map/stage_sum/pallas_call | solution.py:764
  129.1 4.2 %stage_sum.8 = (bf16[2,2,1,2,432,128]{5,4,3,2,1,0:T(8,128)(2,1)}, bf16[1,2,2,2,432,128]{5,4,3,2,1,0:T(8,128)(2,1)}) custom-call(s32[7]{0:T(128)} %stack.27.s_ref.m_ref, bf16[2,2,2,2,576,128]{5,4,3,2,1,0:T(8,128)(2,1)} %get-tuple-element.174.refs_0_, bf16[2,2,2,2,576,128]{5,4,3,2,1,0:T(8,128)(2,1)} %collective-permute-done.6.refs_1_, ...), custom_call_target="tpu_custom_call" | custom-call | flops 1048576 | bytes 65536 | tf_op jit(solution)/shard_map/stage_sum/pallas_call | solution.py:764
  137.6 19.7 %attend_back.3 = (bf16[1024,384]{1,0:T(8,128)(2,1)}, bf16[1024,384]{1,0:T(8,128)(2,1)}, f32[16,128]{1,0:T(8,128)}, bf16[2,2,288,128]{3,2,1,0:T(8,128)(2,1)}, bf16[2,2,288,128]{3,2,1,0:T(8,128)(2,1)}) custom-call(s32[7]{0:T(128)} %stack.27.s_ref.m_ref, bf16[512,1152]{1,0:T(8,128)(2,1)} %get-tuple-element.150.p0, bf16[512,1152]{1,0:T(8,128)(2,1)} %get-tuple-element.151.p1, ...), custom_call_target="tpu_custom_call" | custom-call | flops 1048576 | bytes 65536 | tf_op jit(solution)/shard_map/attend_back/pallas_call | solution.py:352
  158.5 4.1 %stage_sum.9 = (bf16[1,1,2,2,432,128]{5,4,3,2,1,0:T(8,128)(2,1)}, bf16[2,2,1,1,432,128]{5,4,3,2,1,0:T(8,128)(2,1)}, bf16[1,1,2,2,432,128]{5,4,3,2,1,0:T(8,128)(2,1)}) custom-call(s32[7]{0:T(128)} %stack.27.s_ref.m_ref, bf16[2,2,2,2,576,128]{5,4,3,2,1,0:T(8,128)(2,1)} %get-tuple-element.174.refs_0_, ...), custom_call_target="tpu_custom_call" | custom-call | flops 1048576 | bytes 65536 | tf_op jit(solution)/shard_map/stage_sum/pallas_call | solution.py:764
  168.3 19.9 %attend_back.4 = (bf16[1024,384]{1,0:T(8,128)(2,1)}, bf16[1024,384]{1,0:T(8,128)(2,1)}, f32[16,128]{1,0:T(8,128)}, bf16[2,2,288,128]{3,2,1,0:T(8,128)(2,1)}, bf16[2,2,288,128]{3,2,1,0:T(8,128)(2,1)}) custom-call(s32[7]{0:T(128)} %stack.27.s_ref.m_ref, bf16[512,1152]{1,0:T(8,128)(2,1)} %get-tuple-element.150.p0, bf16[512,1152]{1,0:T(8,128)(2,1)} %get-tuple-element.151.p1, ...), custom_call_target="tpu_custom_call" | custom-call | flops 1048576 | bytes 65536 | tf_op jit(solution)/shard_map/attend_back/pallas_call | solution.py:352
  189.4 3.8 %stage_sum.10 = (bf16[1,1,1,2,720,128]{5,4,3,2,1,0:T(8,128)(2,1)}, bf16[2,1,1,1,432,128]{5,4,3,2,1,0:T(8,128)(2,1)}, bf16[1,1,2,1,432,128]{5,4,3,2,1,0:T(8,128)(2,1)}) custom-call(s32[7]{0:T(128)} %stack.27.s_ref.m_ref, bf16[2,2,2,2,576,128]{5,4,3,2,1,0:T(8,128)(2,1)} %get-tuple-element.174.refs_0_, ...), custom_call_target="tpu_custom_call" | custom-call | flops 1048576 | bytes 65536 | tf_op jit(solution)/shard_map/stage_sum/pallas_call | solution.py:764
  196.2 19.7 %attend_back.5 = (bf16[1024,384]{1,0:T(8,128)(2,1)}, bf16[1024,384]{1,0:T(8,128)(2,1)}, f32[16,128]{1,0:T(8,128)}, bf16[2,2,288,128]{3,2,1,0:T(8,128)(2,1)}, bf16[2,2,288,128]{3,2,1,0:T(8,128)(2,1)}) custom-call(s32[7]{0:T(128)} %stack.27.s_ref.m_ref, bf16[512,1152]{1,0:T(8,128)(2,1)} %get-tuple-element.150.p0, bf16[512,1152]{1,0:T(8,128)(2,1)} %get-tuple-element.151.p1, ...), custom_call_target="tpu_custom_call" | custom-call | flops 1048576 | bytes 65536 | tf_op jit(solution)/shard_map/attend_back/pallas_call | solution.py:352
  218.7 3.3 %stage_sum.11 = (bf16[1,1,1,1,720,128]{5,4,3,2,1,0:T(8,128)(2,1)}, bf16[1,1,1,1,432,128]{5,4,3,2,1,0:T(8,128)(2,1)}, bf16[1,1,1,1,432,128]{5,4,3,2,1,0:T(8,128)(2,1)}) custom-call(s32[7]{0:T(128)} %stack.27.s_ref.m_ref, bf16[2,2,2,2,576,128]{5,4,3,2,1,0:T(8,128)(2,1)} %get-tuple-element.174.refs_0_, ...), custom_call_target="tpu_custom_call" | custom-call | flops 1048576 | bytes 65536 | tf_op jit(solution)/shard_map/stage_sum/pallas_call | solution.py:764
  222.9 8.0 %input_grad.2 = (bf16[512,768]{1,0:T(8,128)(2,1)}, f32[8,768]{1,0:T(8,128)}) custom-call(s32[7]{0:T(128)} %stack.27.s_ref.m_ref, bf16[1024,384]{1,0:T(8,128)(2,1)} %get-tuple-element.227.o0, bf16[1024,384]{1,0:T(8,128)(2,1)} %get-tuple-element.228.o1, bf16[1024,384]{1,0:T(8,128)(2,1)} %get-tuple-element.229.o2, ...), custom_call_target="tpu_custom_call" | custom-call | flops 1048576 | bytes 65536 | tf_op jit(solution)/shard_map/input_grad/pallas_call | solution.py:655
  232.7 2.6 stage_sum.12
  236.6 8.0 %input_grad.3 = (bf16[2,512,768]{2,1,0:T(8,128)(2,1)}, f32[24,768]{1,0:T(8,128)}) custom-call(s32[7]{0:T(128)} %stack.27.s_ref.m_ref, bf16[1024,384]{1,0:T(8,128)(2,1)} %get-tuple-element.227.o0, bf16[1024,384]{1,0:T(8,128)(2,1)} %get-tuple-element.228.o1, bf16[1024,384]{1,0:T(8,128)(2,1)} %get-tuple-element.229.o2, ...), custom_call_target="tpu_custom_call" | custom-call | flops 1048576 | bytes 65536 | tf_op jit(solution)/shard_map/input_grad/pallas_call | solution.py:655
  244.7 2.7 collective-permute-start.27
  261.0 3.4 %ffn_sum.1 = (f32[96,768]{1,0:T(8,128)}, f32[24,3072]{1,0:T(8,128)}, f32[24,768]{1,0:T(8,128)}) custom-call(s32[7]{0:T(128)} %stack.27.s_ref.m_ref, bf16[2,2,2,2,576,128]{5,4,3,2,1,0:T(8,128)(2,1)} %get-tuple-element.174.refs_0_, bf16[2,2,2,2,576,128]{5,4,3,2,1,0:T(8,128)(2,1)} %collective-permute-done.6.refs_1_, bf16[2,1,2,2,432,128]{5,4,3,2,1,0:T(8,128)(2,1)} %copy-done.2, ...), custom_call_target="tpu_custom_call" | custom-call | flops 1048576 | bytes 65536 | tf_op jit(solution)/shard_map/ffn_sum/pallas_call | solution.py:764
  264.5 3.9 %collective-permute-start.33 = (f32[24,768]{1,0:T(8,128)S(1)}, f32[24,768]{1,0:T(8,128)S(1)}, u32[]{:S(2)}, u32[]{:S(2)}) collective-permute-start(f32[24,768]{1,0:T(8,128)S(1)} %add.47), channel_id=1, source_target_pairs={{0,16},{4,20},{8,24},{12,28},{16,0},{20,4},{24,8},{28,12},{1,17},{... | collective-permute-start | bytes 221192 | tf_op jit(solution)/shard_map/ppermute | solution.py:804
  268.4 3.0 %qkv_sum.1 = (f32[288,192]{1,0:T(8,128)}, bf16[288,192]{1,0:T(8,128)(2,1)}, bf16[288,192]{1,0:T(8,128)(2,1)}) custom-call(s32[7]{0:T(128)} %stack.27.s_ref.m_ref, bf16[1,1,2,2,288,128]{5,4,3,2,1,0:T(8,128)(2,1)} %bitcast.50, bf16[1,1,2,2,288,128]{5,4,3,2,1,0:T(8,128)(2,1)} %copy-done.12, bf16[1,1,1,2,720,128]{5,4,3,2,1,0:T(8,128)(2,1)} %copy-done.9, ...), custom_call_target="tpu_custom_call" | custom-call | flops 1048576 | bytes 65536 | tf_op jit(solution)/shard_map/qkv_sum/pallas_call | solution.py:764
  273.3 3.2 %collective-permute-start.34 = (f32[24,768]{1,0:T(8,128)S(1)}, f32[24,768]{1,0:T(8,128)S(1)}, u32[]{:S(2)}, u32[]{:S(2)}) collective-permute-start(f32[24,768]{1,0:T(8,128)S(1)} %add.48), channel_id=1, source_target_pairs={{0,2},{1,3},{2,0},{3,1},{4,6},{5,7},{6,4},{7,5},{8,10},{9,11},{10,... | collective-permute-start | bytes 221192 | tf_op jit(solution)/shard_map/ppermute | solution.py:804
  (166 shorter events, 62.5 us)
Async XLA Ops:
  3.1 16.9 %collective-permute-start.1 = (bf16[512,768]{1,0:T(8,128)(2,1)S(1)}, bf16[512,768]{1,0:T(8,128)(2,1)}, u32[]{:S(2)}, u32[]{:S(2)}) collective-permute-start(bf16[512,768]{1,0:T(8,128)(2,1)S(1)} %get-tuple-element.249.x_ref.tok0), channel_id=1, source_target_pairs={{0,1},{1,0},{2,3},{3,2},{4,5},{5,4},{6,7},{7,6},{8,9},{9,8},{10,11... | collective-permute-start | bytes 2359304 | tf_op jit(solution)/shard_map/ppermute | solution.py:879
  3.6 21.8 %collective-permute-start = (bf16[512,768]{1,0:T(8,128)(2,1)}, bf16[512,768]{1,0:T(8,128)(2,1)S(1)}, u32[]{:S(2)}, u32[]{:S(2)}) collective-permute-start(bf16[512,768]{1,0:T(8,128)(2,1)} %get-tuple-element.280), channel_id=1, source_target_pairs={{0,2},{1,3},{2,0},{3,1},{4,6},{5,7},{6,4},{7,5},{8,10},{9,11},{10,... | collective-permute-start | bytes 2359304 | tf_op jit(solution)/shard_map/ppermute | solution.py:882
  38.0 27.4 %collective-permute-start.4 = (bf16[512,768]{1,0:T(8,128)(2,1)S(1)}, bf16[512,768]{1,0:T(8,128)(2,1)S(1)}, u32[]{:S(2)}, u32[]{:S(2)}) collective-permute-start(bf16[512,768]{1,0:T(8,128)(2,1)S(1)} %copy-done.18), channel_id=1, source_target_pairs={{0,2},{1,3},{2,0},{3,1},{4,6},{5,7},{6,4},{7,5},{8,10},{9,11},{10,... | collective-permute-start | bytes 2359304 | tf_op jit(solution)/shard_map/ppermute | solution.py:882
  133.3 24.0 %collective-permute-start.8 = (bf16[2,1,2,2,432,128]{5,4,3,2,1,0:T(8,128)(2,1)}, bf16[2,1,2,2,432,128]{5,4,3,2,1,0:T(8,128)(2,1)S(1)}, u32[]{:S(2)}, u32[]{:S(2)}) collective-permute-start(bf16[2,1,2,2,432,128]{5,4,3,2,1,0:T(8,128)(2,1)} %stage_sum.7), channel_id=1, source_target_pairs={{0,4},{4,0},{8,12},{12,8},{16,20},{20,16},{24,28},{28,24},{1,5},{5... | collective-permute-start | bytes 2654216 | tf_op jit(solution)/shard_map/ppermute | solution.py:804
  134.9 22.5 %collective-permute-start.9 = (bf16[2,2,1,2,432,128]{5,4,3,2,1,0:T(8,128)(2,1)}, bf16[2,2,1,2,432,128]{5,4,3,2,1,0:T(8,128)(2,1)S(1)}, u32[]{:S(2)}, u32[]{:S(2)}) collective-permute-start(bf16[2,2,1,2,432,128]{5,4,3,2,1,0:T(8,128)(2,1)} %get-tuple-element.197), channel_id=1, source_target_pairs={{0,8},{4,12},{8,0},{12,4},{16,24},{20,28},{24,16},{28,20},{1,9},{5... | collective-permute-start | bytes 2654216 | tf_op jit(solution)/shard_map/ppermute | solution.py:804
  136.4 21.5 %collective-permute-start.10 = (bf16[1,2,2,2,432,128]{5,4,3,2,1,0:T(8,128)(2,1)}, bf16[1,2,2,2,432,128]{5,4,3,2,1,0:T(8,128)(2,1)}, u32[]{:S(2)}, u32[]{:S(2)}) collective-permute-start(bf16[1,2,2,2,432,128]{5,4,3,2,1,0:T(8,128)(2,1)} %get-tuple-element.198), channel_id=1, source_target_pairs={{0,2},{1,3},{2,0},{3,1},{4,6},{5,7},{6,4},{7,5},{8,10},{9,11},{10,... | collective-permute-start | bytes 2654216 | tf_op jit(solution)/shard_map/ppermute | solution.py:804
  162.6 30.5 %collective-permute-start.11 = (bf16[1024,384]{1,0:T(8,128)(2,1)}, bf16[1024,384]{1,0:T(8,128)(2,1)}, u32[]{:S(2)}, u32[]{:S(2)}) collective-permute-start(bf16[1024,384]{1,0:T(8,128)(2,1)} %get-tuple-element.206), channel_id=1, source_target_pairs={{0,1},{1,0},{2,3},{3,2},{4,5},{5,4},{6,7},{7,6},{8,9},{9,8},{10,11... | collective-permute-start | bytes 2359304 | tf_op jit(solution)/shard_map/ppermute | solution.py:879
  162.7 25.4 %collective-permute-start.12 = (bf16[1,1,2,2,432,128]{5,4,3,2,1,0:T(8,128)(2,1)}, bf16[1,1,2,2,432,128]{5,4,3,2,1,0:T(8,128)(2,1)S(1)}, u32[]{:S(2)}, u32[]{:S(2)}) collective-permute-start(bf16[1,1,2,2,432,128]{5,4,3,2,1,0:T(8,128)(2,1)} %get-tuple-element.208), channel_id=1, source_target_pairs={{0,2},{1,3},{2,0},{3,1},{4,6},{5,7},{6,4},{7,5},{8,10},{9,11},{10,... | collective-permute-start | bytes 1327112 | tf_op jit(solution)/shard_map/ppermute | solution.py:804
  163.6 24.5 %collective-permute-start.14 = (bf16[2,2,1,1,432,128]{5,4,3,2,1,0:T(8,128)(2,1)}, bf16[2,2,1,1,432,128]{5,4,3,2,1,0:T(8,128)(2,1)S(1)}, u32[]{:S(2)}, u32[]{:S(2)}) collective-permute-start(bf16[2,2,1,1,432,128]{5,4,3,2,1,0:T(8,128)(2,1)} %get-tuple-element.211), channel_id=1, source_target_pairs={{0,16},{4,20},{8,24},{12,28},{16,0},{20,4},{24,8},{28,12},{1,17},{... | collective-permute-start | bytes 1327112 | tf_op jit(solution)/shard_map/ppermute | solution.py:804
  166.2 22.0 %collective-permute-start.15 = (bf16[1,1,2,2,432,128]{5,4,3,2,1,0:T(8,128)(2,1)}, bf16[1,1,2,2,432,128]{5,4,3,2,1,0:T(8,128)(2,1)S(1)}, u32[]{:S(2)}, u32[]{:S(2)}) collective-permute-start(bf16[1,1,2,2,432,128]{5,4,3,2,1,0:T(8,128)(2,1)} %get-tuple-element.212), channel_id=1, source_target_pairs={{0,4},{4,0},{8,12},{12,8},{16,20},{20,16},{24,28},{28,24},{1,5},{5... | collective-permute-start | bytes 1327112 | tf_op jit(solution)/shard_map/ppermute | solution.py:804
  166.8 21.4 %collective-permute-start.13 = (bf16[1,1,2,2,288,128]{5,4,3,2,1,0:T(8,128)(2,1)}, bf16[1,1,2,2,288,128]{5,4,3,2,1,0:T(8,128)(2,1)S(1)}, u32[]{:S(2)}, u32[]{:S(2)}) collective-permute-start(bf16[1,1,2,2,288,128]{5,4,3,2,1,0:T(8,128)(2,1)} %bitcast.58), channel_id=1, source_target_pairs={{0,4},{4,0},{8,12},{12,8},{16,20},{20,16},{24,28},{28,24},{1,5},{5... | collective-permute-start | bytes 884744 | tf_op jit(solution)/shard_map/ppermute | solution.py:804
  193.2 22.8 %collective-permute-start.16 = (bf16[1024,384]{1,0:T(8,128)(2,1)}, bf16[1024,384]{1,0:T(8,128)(2,1)S(1)}, u32[]{:S(2)}, u32[]{:S(2)}) collective-permute-start(bf16[1024,384]{1,0:T(8,128)(2,1)} %get-tuple-element.221), channel_id=1, source_target_pairs={{0,1},{1,0},{2,3},{3,2},{4,5},{5,4},{6,7},{7,6},{8,9},{9,8},{10,11... | collective-permute-start | bytes 2359304 | tf_op jit(solution)/shard_map/ppermute | solution.py:879
  193.3 22.7 %collective-permute-start.17 = (bf16[512,768]{1,0:T(8,128)(2,1)}, bf16[512,768]{1,0:T(8,128)(2,1)}, u32[]{:S(2)}, u32[]{:S(2)}) collective-permute-start(bf16[512,768]{1,0:T(8,128)(2,1)} %get-tuple-element.222), channel_id=1, source_target_pairs={{0,2},{1,3},{2,0},{3,1},{4,6},{5,7},{6,4},{7,5},{8,10},{9,11},{10,... | collective-permute-start | bytes 2359304 | tf_op jit(solution)/shard_map/ppermute | solution.py:882
  194.5 21.4 %collective-permute-start.18 = (bf16[1,1,1,2,720,128]{5,4,3,2,1,0:T(8,128)(2,1)}, bf16[1,1,1,2,720,128]{5,4,3,2,1,0:T(8,128)(2,1)S(1)}, u32[]{:S(2)}, u32[]{:S(2)}) collective-permute-start(bf16[1,1,1,2,720,128]{5,4,3,2,1,0:T(8,128)(2,1)} %get-tuple-element.223), channel_id=1, source_target_pairs={{0,8},{4,12},{8,0},{12,4},{16,24},{20,28},{24,16},{28,20},{1,9},{5... | collective-permute-start | bytes 1105928 | tf_op jit(solution)/shard_map/ppermute | solution.py:804
  195.0 20.9 %collective-permute-start.19 = (bf16[2,1,1,1,432,128]{5,4,3,2,1,0:T(8,128)(2,1)}, bf16[2,1,1,1,432,128]{5,4,3,2,1,0:T(8,128)(2,1)S(1)}, u32[]{:S(2)}, u32[]{:S(2)}) collective-permute-start(bf16[2,1,1,1,432,128]{5,4,3,2,1,0:T(8,128)(2,1)} %get-tuple-element.224), channel_id=1, source_target_pairs={{0,4},{4,0},{8,12},{12,8},{16,20},{20,16},{24,28},{28,24},{1,5},{5... | collective-permute-start | bytes 663560 | tf_op jit(solution)/shard_map/ppermute | solution.py:804
  195.6 20.3 %collective-permute-start.20 = (bf16[1,1,2,1,432,128]{5,4,3,2,1,0:T(8,128)(2,1)}, bf16[1,1,2,1,432,128]{5,4,3,2,1,0:T(8,128)(2,1)S(1)}, u32[]{:S(2)}, u32[]{:S(2)}) collective-permute-start(bf16[1,1,2,1,432,128]{5,4,3,2,1,0:T(8,128)(2,1)} %get-tuple-element.225), channel_id=1, source_target_pairs={{0,16},{4,20},{8,24},{12,28},{16,0},{20,4},{24,8},{28,12},{1,17},{... | collective-permute-start | bytes 663560 | tf_op jit(solution)/shard_map/ppermute | solution.py:804
  216.7 15.4 %collective-permute-start.22 = (bf16[1,1,2,2,288,128]{5,4,3,2,1,0:T(8,128)(2,1)}, bf16[1,1,2,2,288,128]{5,4,3,2,1,0:T(8,128)(2,1)}, u32[]{:S(2)}, u32[]{:S(2)}) collective-permute-start(bf16[1,1,2,2,288,128]{5,4,3,2,1,0:T(8,128)(2,1)} %bitcast.56), channel_id=1, source_target_pairs={{0,4},{4,0},{8,12},{12,8},{16,20},{20,16},{24,28},{28,24},{1,5},{5... | collective-permute-start | bytes 884744 | tf_op jit(solution)/shard_map/ppermute | solution.py:804
  218.1 14.7 %collective-permute-start.23 = (bf16[1,1,2,2,288,128]{5,4,3,2,1,0:T(8,128)(2,1)}, bf16[1,1,2,2,288,128]{5,4,3,2,1,0:T(8,128)(2,1)}, u32[]{:S(2)}, u32[]{:S(2)}) collective-permute-start(bf16[1,1,2,2,288,128]{5,4,3,2,1,0:T(8,128)(2,1)} %bitcast.57), channel_id=1, source_target_pairs={{0,4},{4,0},{8,12},{12,8},{16,20},{20,16},{24,28},{28,24},{1,5},{5... | collective-permute-start | bytes 884744 | tf_op jit(solution)/shard_map/ppermute | solution.py:804
  230.9 33.5 %collective-permute-start.32 = (bf16[512,768]{1,0:T(8,128)(2,1)}, bf16[512,768]{1,0:T(8,128)(2,1)S(1)}, u32[]{:S(2)}, u32[]{:S(2)}) collective-permute-start(bf16[512,768]{1,0:T(8,128)(2,1)} %get-tuple-element.264), channel_id=1, source_target_pairs={{0,2},{1,3},{2,0},{3,1},{4,6},{5,7},{6,4},{7,5},{8,10},{9,11},{10,... | collective-permute-start | bytes 2359304 | tf_op jit(solution)/shard_map/ppermute | solution.py:882
  235.3 14.5 %collective-permute-start.25 = (bf16[1,1,1,2,576,128]{5,4,3,2,1,0:T(8,128)(2,1)}, bf16[1,1,1,2,576,128]{5,4,3,2,1,0:T(8,128)(2,1)S(1)}, u32[]{:S(2)}, u32[]{:S(2)}) collective-permute-start(bf16[1,1,1,2,576,128]{5,4,3,2,1,0:T(8,128)(2,1)} %stage_sum.12), channel_id=1, source_target_pairs={{0,8},{4,12},{8,0},{12,4},{16,24},{20,28},{24,16},{28,20},{1,9},{5... | collective-permute-start | bytes 884744 | tf_op jit(solution)/shard_map/ppermute | solution.py:804
  244.7 11.9 %collective-permute-start.27 = (bf16[1,1,1,1,720,128]{5,4,3,2,1,0:T(8,128)(2,1)S(1)}, bf16[1,1,1,1,720,128]{5,4,3,2,1,0:T(8,128)(2,1)S(1)}, u32[]{:S(2)}, u32[]{:S(2)}) collective-permute-start(bf16[1,1,1,1,720,128]{5,4,3,2,1,0:T(8,128)(2,1)S(1)} %copy-done.30), channel_id=1, source_target_pairs={{0,16},{4,20},{8,24},{12,28},{16,0},{20,4},{24,8},{28,12},{1,17},{... | collective-permute-start | bytes 552968 | tf_op jit(solution)/shard_map/ppermute | solution.py:804
  254.3 10.2 %collective-permute-start.31 = (bf16[1,1,1,1,576,128]{5,4,3,2,1,0:T(8,128)(2,1)}, bf16[1,1,1,1,576,128]{5,4,3,2,1,0:T(8,128)(2,1)S(1)}, u32[]{:S(2)}, u32[]{:S(2)}) collective-permute-start(bf16[1,1,1,1,576,128]{5,4,3,2,1,0:T(8,128)(2,1)} %stage_sum.13), channel_id=1, source_target_pairs={{0,16},{4,20},{8,24},{12,28},{16,0},{20,4},{24,8},{28,12},{1,17},{... | collective-permute-start | bytes 442376 | tf_op jit(solution)/shard_map/ppermute | solution.py:804
  256.6 7.9 %collective-permute-start.30 = (f32[24,768]{1,0:T(8,128)S(1)}, f32[24,768]{1,0:T(8,128)S(1)}, u32[]{:S(2)}, u32[]{:S(2)}) collective-permute-start(f32[24,768]{1,0:T(8,128)S(1)} %add.46), channel_id=1, source_target_pairs={{0,8},{4,12},{8,0},{12,4},{16,24},{20,28},{24,16},{28,20},{1,9},{5... | collective-permute-start | bytes 221192 | tf_op jit(solution)/shard_map/ppermute | solution.py:804
  264.5 8.7 %collective-permute-start.33 = (f32[24,768]{1,0:T(8,128)S(1)}, f32[24,768]{1,0:T(8,128)S(1)}, u32[]{:S(2)}, u32[]{:S(2)}) collective-permute-start(f32[24,768]{1,0:T(8,128)S(1)} %add.47), channel_id=1, source_target_pairs={{0,16},{4,20},{8,24},{12,28},{16,0},{20,4},{24,8},{28,12},{1,17},{... | collective-permute-start | bytes 221192 | tf_op jit(solution)/shard_map/ppermute | solution.py:804
  (46 other events, 222.6 us)
